TPU v7x, 128 devices: a whole 4x4x4 slice. The times are simulated.
128 devices in a mesh: rows: 32 (over x, z, core), cols: 4 (over y).
Axes of the slice: x: 4, y: 4, z: 4, core: 2. Of those that a mesh axis runs over, the one named last changes fastest.
Arguments:
- basis: bfloat16 [262144, 512], P('rows', 'cols'), may hold values from -6 to 6
- lower: bfloat16 [1024, 256, 256], P('rows'), may hold values from -0.375 to 0.375
- diag: bfloat16 [1024, 256, 256], P('rows'), may hold values from -0.375 to 0.375
- upper: bfloat16 [1024, 256, 256], P('rows'), may hold values from -0.375 to 0.375
- inverse: bfloat16 [1024, 256, 256], P('rows'), may hold values from -0.375 to 0.375
Outputs:
- ortho: bfloat16 [262144, 512], P('rows', 'cols')
- projected: float32 [512, 512], P(None, 'cols')
All inputs are finite; a program needn't handle non-finite values.
Results may differ from a plain program's by a relative error of at most 0.0085.
Values may be sent and summed in bfloat16 or wider, within the bound.
No kernel may reach another device: no remote copies, remote signals or barrier semaphores. Data moves between devices by JAX's collectives and lax.ppermute only.
A program may use at most 128 MiB of HBM per device.

v0:
```python
import functools

import jax
import jax.numpy as jnp
from jax import lax
from jax.experimental import pallas as pl
from jax.experimental.pallas import tpu as pltpu
from jax.sharding import PartitionSpec as P

F32 = jnp.float32
BF16 = jnp.bfloat16
HI = lax.Precision.HIGHEST
X, Z, CORE, Y = 4, 4, 2, 4
PARTS = 4
LIMIT = 56 << 20


def dot(a, b, ca=1, cb=0, precision=None):
    return lax.dot_general(
        a, b, (((ca,), (cb,)), ((), ())), precision=precision, preferred_element_type=F32
    )


def cost(flops, bytes_accessed):
    return pl.CostEstimate(flops=flops, transcendentals=0, bytes_accessed=bytes_accessed)


def vmem():
    return pl.BlockSpec(memory_space=pltpu.VMEM)


def shape(dims, dtype):
    return jax.ShapeDtypeStruct(dims, dtype)


def over_rows(move):
    pairs = []
    for x in range(X):
        for z in range(Z):
            for core in range(CORE):
                tx, tz, tc = move(x, z, core)
                source = (x * Z + z) * CORE + core
                pairs.append((source, ((tx % X) * Z + tz % Z) * CORE + tc % CORE))
    return pairs


def flip(value):
    return lax.ppermute(value, "rows", over_rows(lambda x, z, c: (x, z, c + 1)))


PLANE = [[(x * Z + z) * CORE + c for x in range(X) for z in range(Z)] for c in range(CORE)]


def plane(value):
    return lax.all_to_all(value, "rows", 0, 0, tiled=True, axis_index_groups=PLANE)


def along_cols(value, s):
    return lax.ppermute(value, "cols", [(i, (i + s) % Y) for i in range(Y)])


def chain(value, step):
    count = X * Z * CORE * Y
    return lax.ppermute(
        value,
        ("rows", "cols"),
        [(i, i + step) for i in range(count) if 0 <= i + step < count],
    )


def total_of(pieces):
    total = jnp.sum(plane(pieces), axis=0)
    r1, r2, r3 = (along_cols(total, s) for s in (1, 2, 3))
    return (total + r2) + (r1 + r3)


def gathered(piece):
    mine = plane(jnp.broadcast_to(piece[None], (X * Z, *piece.shape)))
    return mine, flip(mine)


def pack_kernel(keep, got, out):
    groups, rows, width = out.shape
    q = rows // Y
    for p in range(groups):
        for d in range(Y):
            at = slice(d * width, (d + 1) * width)
            out[p, d * q : (d + 1) * q, :] = (
                keep[p * q : (p + 1) * q, at] + got[p * q : (p + 1) * q, at]
            )


def pack(keep, got):
    groups = X * Z
    width = keep.shape[1] // Y
    return pl.pallas_call(
        pack_kernel,
        out_shape=shape((groups, keep.shape[0] * Y // groups, width), F32),
        in_specs=[vmem()] * 2,
        out_specs=vmem(),
        cost_estimate=cost(keep.size, 12 * keep.size),
        name="pack",
    )(keep, got)


def apply_blocks(v, lower, diag, upper, inverse, out):
    count, size, _ = diag.shape
    mixed = [
        (dot(lower[k], v[k]) + dot(diag[k], v[k + 1]) + dot(upper[k], v[k + 2])).astype(BF16)
        for k in range(count)
    ]
    for k in range(count):
        out[k * size : (k + 1) * size, :] = dot(inverse[k], mixed[k]).astype(BF16)


def op_kernel(meta, prev, cur, nxt, low, high, lower, diag, upper, inverse, out, *, j, per, count):
    size = diag.shape[1]
    first = lax.rem(meta[0] + j, Y) * (count // Y) + pl.program_id(0) * per
    v = [jnp.where(first == 0, low[...], prev[...])]
    v += [cur[k * size : (k + 1) * size, :] for k in range(per)]
    v += [jnp.where(first + per == count, high[...], nxt[...])]
    apply_blocks(v, lower, diag, upper, inverse, out)


def op_chunk(meta, basis, low, high, lower, diag, upper, inverse, j):
    count, size, _ = diag.shape
    width = basis.shape[1]
    per = 4
    steps = count // Y // per

    def block(i, m):
        return lax.rem(m[0] + j, Y) * steps + i

    def at(i, m):
        return (block(i, m), 0)

    def weights(i, m):
        return (block(i, m), 0, 0)

    mat = pl.BlockSpec((per, size, size), weights)
    return pl.pallas_call(
        functools.partial(op_kernel, j=j, per=per, count=count),
        out_shape=shape((count // Y * size, width), BF16),
        grid_spec=pltpu.PrefetchScalarGridSpec(
            num_scalar_prefetch=1,
            grid=(steps,),
            in_specs=[
                pl.BlockSpec((size, width), lambda i, m: (jnp.maximum(block(i, m) * per - 1, 0), 0)),
                pl.BlockSpec((per * size, width), at),
                pl.BlockSpec(
                    (size, width), lambda i, m: (jnp.minimum(block(i, m) * per + per, count - 1), 0)
                ),
                pl.BlockSpec((size, width), lambda i, m: (0, 0)),
                pl.BlockSpec((size, width), lambda i, m: (0, 0)),
                mat,
                mat,
                mat,
                mat,
            ],
            out_specs=pl.BlockSpec((per * size, width), lambda i, m: (i, 0)),
        ),
        cost_estimate=cost(8 * size * size * width * count // Y, 10 * size * size * count // Y),
        compiler_params=pltpu.CompilerParams(vmem_limit_bytes=LIMIT),
        name=f"op{j}",
    )(meta, basis, basis, basis, low, high, lower, diag, upper, inverse)


def gram_kernel(meta, p0, p1, p2, p3, wide, top, bottom, keep, send, full, flat, *, size):
    width = p0.shape[1]
    for s, piece in enumerate((p0, p1, p2, p3)):
        at = lax.rem(meta[0] + Y - s, Y) * width
        wide[:, pl.ds(pl.multiple_of(at, width), width)] = piece[...]
    rows = wide.shape[0]
    top[...] = wide[0:size, :]
    bottom[...] = wide[rows - size : rows, :]
    full[...] = dot(wide[...], wide[...], 0, 0)
    n = 0
    for a in range(Y):
        for b in range(a, Y):
            flat[n * width : (n + 1) * width, :] = full[
                a * width : (a + 1) * width, b * width : (b + 1) * width
            ]
            n += 1
    half = flat.shape[0] // 2
    core = meta[1]
    keep[...] = flat[pl.ds(pl.multiple_of(core * half, 8), half), :]
    send[...] = flat[pl.ds(pl.multiple_of((1 - core) * half, 8), half), :]


def gram_of(meta, pieces, size):
    rows, width = pieces[0].shape
    k = Y * width
    n = Y * (Y + 1) // 2 * width
    return pl.pallas_call(
        functools.partial(gram_kernel, size=size),
        out_shape=(
            shape((rows, k), BF16),
            shape((size, k), BF16),
            shape((size, k), BF16),
            shape((n // 2, width), F32),
            shape((n // 2, width), F32),
        ),
        grid_spec=pltpu.PrefetchScalarGridSpec(
            num_scalar_prefetch=1,
            in_specs=[vmem()] * 4,
            out_specs=(vmem(),) * 5,
            scratch_shapes=[pltpu.VMEM((k, k), F32), pltpu.VMEM((n, width), F32)],
        ),
        cost_estimate=cost(2 * rows * k * k, 4 * rows * k + 4 * k * k),
        compiler_params=pltpu.CompilerParams(vmem_limit_bytes=LIMIT),
        name="gram",
    )(meta, *pieces)


def moment_kernel(meta, prev, cur, nxt, low, high, lower, diag, upper, inverse, keep, send, acc, image):
    i = pl.program_id(0)
    last = pl.num_programs(0) - 1
    per, size, _ = diag.shape
    v = [jnp.where(i == 0, low[...], prev[...])]
    v += [cur[k * size : (k + 1) * size, :] for k in range(per)]
    v += [jnp.where(i == last, high[...], nxt[...])]
    apply_blocks(v, lower, diag, upper, inverse, image)
    term = dot(cur[...], image[...], 0, 0)

    @pl.when(i == 0)
    def _():
        acc[...] = term

    @pl.when(i > 0)
    def _():
        acc[...] += term

    @pl.when(i == last)
    def _():
        half = acc.shape[0] // 2
        core = meta[1]
        keep[...] = acc[pl.ds(pl.multiple_of(core * half, 8), half), :]
        send[...] = acc[pl.ds(pl.multiple_of((1 - core) * half, 8), half), :]


def moment_of(meta, wide, low, high, lower, diag, upper, inverse):
    count, size, _ = diag.shape
    per = 4
    steps = count // Y // per
    blocks = steps * per
    k = wide.shape[1]
    mat = pl.BlockSpec((per, size, size), lambda i, m: (m[0] * steps + i, 0, 0))
    out = pl.BlockSpec((k // 2, k), lambda i, m: (0, 0))
    return pl.pallas_call(
        moment_kernel,
        out_shape=(shape((k // 2, k), F32), shape((k // 2, k), F32)),
        grid_spec=pltpu.PrefetchScalarGridSpec(
            num_scalar_prefetch=1,
            grid=(steps,),
            in_specs=[
                pl.BlockSpec((size, k), lambda i, m: (jnp.maximum(i * per - 1, 0), 0)),
                pl.BlockSpec((per * size, k), lambda i, m: (i, 0)),
                pl.BlockSpec((size, k), lambda i, m: (jnp.minimum(i * per + per, blocks - 1), 0)),
                pl.BlockSpec((size, k), lambda i, m: (0, 0)),
                pl.BlockSpec((size, k), lambda i, m: (0, 0)),
                mat,
                mat,
                mat,
                mat,
            ],
            out_specs=(out, out),
            scratch_shapes=[pltpu.VMEM((k, k), F32), pltpu.VMEM((per * size, k), BF16)],
        ),
        cost_estimate=cost(blocks * size * k * (8 * size + 2 * k), 4 * blocks * size * k),
        compiler_params=pltpu.CompilerParams(vmem_limit_bytes=LIMIT),
        name="moment",
    )(meta, wide, wide, wide, low, high, lower, diag, upper, inverse)


def eliminate(a):
    groups = len(a)
    wide = (8, 8 * groups)
    sub = lax.broadcasted_iota(jnp.int32, wide, 0)
    lane = lax.broadcasted_iota(jnp.int32, wide, 1)
    a = list(a)

    def column(value, k):
        return jnp.broadcast_to(value[:, k : k + 1], wide)

    def row(value, k):
        return jnp.broadcast_to(value[k : k + 1, :], wide)

    done = []
    for g in range(groups):
        base = 8 * g
        cols = [column(a[g], base + k) for k in range(8)]
        d = [[row(cols[k], i) if i >= k else None for k in range(8)] for i in range(8)]
        low = [[None] * 8 for _ in range(8)]
        scale = [None] * 8
        for k in range(8):
            scale[k] = lax.rsqrt(d[k][k])
            ratio = 1.0 / d[k][k]
            for i in range(k + 1, 8):
                low[i][k] = d[i][k] * scale[k]
                for j in range(k + 1, i + 1):
                    d[i][j] = d[i][j] - (d[i][k] * d[j][k]) * ratio

        def forward(value):
            out = []
            for k in range(8):
                x = value[k]
                for j in range(k):
                    x = x - low[k][j] * out[j]
                out.append(x * scale[k])
            return out

        inside = (lane >= base) & (lane < base + 8)
        own = jnp.where(inside, jnp.where(lane - base == sub, 1.0, 0.0), a[g])
        r = forward([row(own, k) for k in range(8)])
        w = [None] * 8
        if g + 2 < groups:
            for k in reversed(range(8)):
                x = r[k]
                for j in range(k + 1, 8):
                    x = x - low[j][k] * w[j]
                w[k] = x * scale[k]
        for h in range(g + 1, groups):
            c = [column(a[h], base + k) for k in range(8)]
            if h == g + 1:
                c = forward(c)
            x = jnp.where(inside, 0.0, a[h])
            for k in range(8):
                x = x - c[k] * (r if h == g + 1 else w)[k]
            a[h] = x
        rows = r[0]
        for k in range(1, 8):
            rows = jnp.where(sub == k, r[k], rows)
        done.append(jnp.where(lane <= sub + base, rows, 0.0))
    return done


def factor_kernel(meta, mine, other, out, w, inv, flat):
    n = w.shape[0]
    nb = n // Y
    groups = mine.shape[0]
    tall = flat.shape[0] // (2 * groups)
    for which, half in ((mine, meta[1]), (other, 1 - meta[1])):
        for p in range(groups):
            at = pl.multiple_of((half * groups + p) * tall, 8)
            flat[pl.ds(at, tall), :] = which[p, 0:tall, :]
    at = 0
    for a in range(Y):
        for b in range(a, Y):
            block = flat[at : at + nb, :]
            w[a * nb : (a + 1) * nb, b * nb : (b + 1) * nb] = block
            if a != b:
                w[b * nb : (b + 1) * nb, a * nb : (a + 1) * nb] = block.T
            at += nb
    def trail(p, l21, r12):
        lo, hi = p * nb, (p + 1) * nb
        w[hi:n, hi:n] = w[hi:n, hi:n] - dot(l21, r12, precision=HI)
        new = dot(l21, inv[lo:hi, 0:hi], precision=HI)
        if p:
            inv[hi:n, 0:lo] = inv[hi:n, 0:lo] - new[:, 0:lo]
        inv[hi:n, lo:hi] = -new[:, lo:hi]

    diag = w[0:nb, 0:nb]
    held = None
    for p in range(Y):
        lo, hi = p * nb, (p + 1) * nb
        li = jnp.concatenate(
            eliminate([diag[8 * g : 8 * g + 8, :] for g in range(nb // 8)]), axis=0
        )
        if held:
            trail(p - 1, *held)
            inv[lo:hi, 0:lo] = dot(li, inv[lo:hi, 0:lo], precision=HI)
        inv[lo:hi, lo:hi] = li
        if hi < n:
            inv[lo:hi, hi:n] = jnp.zeros((nb, n - hi), F32)
            held = (dot(w[hi:n, lo:hi], li, 1, 1, HI), dot(li, w[lo:hi, hi:n], precision=HI))
            diag = w[hi : hi + nb, hi : hi + nb] - dot(held[0][0:nb], held[1][:, 0:nb], precision=HI)
    out[...] = inv[...].astype(BF16)


def factor_of(meta, mine, other):
    width = mine.shape[2]
    k = Y * width
    return pl.pallas_call(
        factor_kernel,
        out_shape=shape((k, k), BF16),
        grid_spec=pltpu.PrefetchScalarGridSpec(
            num_scalar_prefetch=1,
            in_specs=[vmem()] * 2,
            out_specs=vmem(),
            scratch_shapes=[
                pltpu.VMEM((k, k), F32),
                pltpu.VMEM((k, k), F32),
                pltpu.VMEM((Y * (Y + 1) // 2 * width, width), F32),
            ],
        ),
        cost_estimate=cost(k * k * k, 12 * k * k),
        compiler_params=pltpu.CompilerParams(vmem_limit_bytes=LIMIT),
        name="factor",
    )(meta, mine, other)


def ortho_kernel(meta, linv, wide, *refs):
    outs, full = refs[:Y], refs[Y]
    width = outs[0].shape[1]
    full[...] = dot(wide[...], linv[...], 1, 1).astype(BF16)
    for t in range(Y):
        at = pl.multiple_of(lax.rem(meta[0] + t, Y) * width, width)
        outs[t][...] = full[:, pl.ds(at, width)]


def ortho_of(meta, linv, wide):
    rows, k = wide.shape
    width = k // Y
    return pl.pallas_call(
        ortho_kernel,
        out_shape=[shape((rows, width), BF16)] * Y,
        grid_spec=pltpu.PrefetchScalarGridSpec(
            num_scalar_prefetch=1,
            in_specs=[vmem()] * 2,
            out_specs=[vmem()] * Y,
            scratch_shapes=[pltpu.VMEM((rows, k), BF16)],
        ),
        cost_estimate=cost(2 * rows * k * k, 4 * rows * k),
        compiler_params=pltpu.CompilerParams(vmem_limit_bytes=LIMIT),
        name="ortho",
    )(meta, linv, wide)


def join_kernel(meta, *refs):
    parts, out = refs[:Y], refs[Y]
    rows = parts[0].shape[0]
    for t in range(Y):
        at = pl.multiple_of(lax.rem(meta[0] + Y - t, Y) * rows, rows)
        out[pl.ds(at, rows), :] = parts[t][...]


def join(meta, parts):
    rows, width = parts[0].shape
    return pl.pallas_call(
        join_kernel,
        out_shape=shape((Y * rows, width), BF16),
        grid_spec=pltpu.PrefetchScalarGridSpec(
            num_scalar_prefetch=1, in_specs=[vmem()] * Y, out_specs=vmem()
        ),
        cost_estimate=cost(0, 4 * Y * rows * width),
        compiler_params=pltpu.CompilerParams(vmem_limit_bytes=LIMIT),
        name="join",
    )(meta, *parts)


def thirds(x):
    a = x.astype(BF16)
    x = x - a.astype(F32)
    b = x.astype(BF16)
    return a, b, (x - b.astype(F32)).astype(BF16)


def tail_kernel(meta, linv, moment, out):
    q, width = out.shape
    rows = linv[pl.ds(pl.multiple_of(meta[0] * width, width), width), :]
    out[...] = sum(
        dot(part, rows[:, d * width : (d + 1) * width], 1, 1)
        for d in range(Y)
        for part in thirds(moment[d * q : (d + 1) * q, :])
    )


def tail_of(meta, linv, moment):
    rows, width = moment.shape
    return pl.pallas_call(
        tail_kernel,
        out_shape=shape((rows // Y, width), F32),
        grid_spec=pltpu.PrefetchScalarGridSpec(
            num_scalar_prefetch=1, in_specs=[vmem()] * 2, out_specs=vmem()
        ),
        cost_estimate=cost(6 * rows * width * width, 2 * linv.size),
        name="tail",
    )(meta, linv, moment)


def project_kernel(meta, linv, mine, other, out, full):
    groups, q, _ = mine.shape
    for which, half in ((mine, meta[1]), (other, 1 - meta[1])):
        for p in range(groups):
            full[pl.ds(pl.multiple_of((half * groups + p) * q, q), q), :] = which[p]
    out[...] = sum(dot(linv[...], part) for part in thirds(full[...]))


def project_of(meta, linv, mine, other):
    k = linv.shape[0]
    width = k // Y
    return pl.pallas_call(
        project_kernel,
        out_shape=shape((k, width), F32),
        grid_spec=pltpu.PrefetchScalarGridSpec(
            num_scalar_prefetch=1,
            in_specs=[vmem()] * 3,
            out_specs=vmem(),
            scratch_shapes=[pltpu.VMEM((k, width), F32)],
        ),
        cost_estimate=cost(6 * k * k * width, 4 * k * k),
        name="project",
    )(meta, linv, mine, other)


def shards(basis, lower, diag, upper, inverse):
    count, size, _ = diag.shape
    r = lax.axis_index("rows")
    c = lax.axis_index("cols")
    meta = jnp.stack([c, lax.rem(r, CORE)]).astype(jnp.int32)

    rows = X * Z * CORE
    forward = [(i, i + 1) for i in range(rows - 1)]
    low = lax.ppermute(basis[-size:], "rows", forward)
    high = lax.ppermute(basis[:size], "rows", [(b, a) for a, b in forward])

    mats = (lower, diag, upper, inverse)
    work = {j: op_chunk(meta, basis, low, high, *mats, j) for j in (2, 1, 3, 0)}
    near = [work[0]] + [along_cols(work[s], s) for s in (1, 2, 3)]
    wide, top, bottom, keep, send = gram_of(meta, near, size)

    half = keep + flip(send)
    gram = total_of(half.reshape(X * Z, -1, half.shape[1]))
    linv = factor_of(meta, *gathered(gram))
    parts = ortho_of(meta, linv, wide)
    ortho = join(meta, [parts[0]] + [along_cols(parts[t], t) for t in (1, 2, 3)])

    before = chain(bottom, 1)
    after = chain(top, -1)
    keep, send = moment_of(meta, wide, before, after, *mats)
    moment = total_of(pack(keep, flip(send)))
    projected = project_of(meta, linv, *gathered(tail_of(meta, linv, moment)))
    return ortho, projected


def solution(mesh):
    in_specs = (
        P("rows", "cols"),
        P("rows", None, None),
        P("rows", None, None),
        P("rows", None, None),
        P("rows", None, None),
    )
    out_specs = (P("rows", "cols"), P(None, "cols"))
    return jax.shard_map(shards, mesh=mesh, in_specs=in_specs, out_specs=out_specs, check_vma=False)
```

profile of v0, /device:TPU:1, one launch (start us, length us, event | category | flops | bytes accessed | tf_op | source)
XLA Modules:
  0.0 182.7 jit_solution(16308612265952817634)
XLA Ops:
  0.6 0.9 fusion
  1.5 4.9 %collective-permute-start = (bf16[256,128]{1,0:T(8,128)(2,1)S(1)}, bf16[256,128]{1,0:T(8,128)(2,1)S(1)}, u32[]{:S(2)}, u32[]{:S(2)}) collective-permute-start(bf16[256,128]{1,0:T(8,128)(2,1)S(1)} %get-tuple-element.25), channel_id=1, source_target_pairs={{0,4},{4,8},{8,12},{12,16},{16,20},{20,24},{24,28},{28,32},{32,36}... | collective-permute-start | bytes 196616 | tf_op jit(solution)/shard_map/ppermute | solution.py:514
  6.5 1.9 %collective-permute-start.1 = (bf16[256,128]{1,0:T(8,128)(2,1)S(1)}, bf16[256,128]{1,0:T(8,128)(2,1)S(1)}, u32[]{:S(2)}, u32[]{:S(2)}) collective-permute-start(bf16[256,128]{1,0:T(8,128)(2,1)S(1)} %get-tuple-element.24), channel_id=1, source_target_pairs={{4,0},{8,4},{12,8},{16,12},{20,16},{24,20},{28,24},{32,28},{36,32}... | collective-permute-start | bytes 196616 | tf_op jit(solution)/shard_map/ppermute | solution.py:515
  9.0 3.1 %collective-permute-done.1.high = bf16[256,128]{1,0:T(8,128)(2,1)S(1)} collective-permute-done((bf16[256,128]{1,0:T(8,128)(2,1)S(1)}, bf16[256,128]{1,0:T(8,128)(2,1)S(1)}, u32[]{:S(2)}, u32[]{:S(2)}) %collective-permute-start.1) | collective-permute-done | bytes 65568 | tf_op jit(solution)/shard_map/ppermute | solution.py:515
  12.7 4.7 %op1.1 = bf16[2048,128]{1,0:T(8,128)(2,1)} custom-call(s32[2]{0:T(128)} %pad_add_fusion.meta, bf16[8192,128]{1,0:T(8,128)(2,1)} %nxt.7, bf16[8192,128]{1,0:T(8,128)(2,1)} %nxt.7, bf16[8192,128]{1,0:T(8,128)(2,1)} %nxt.7, bf16[256,128]{1,0:T(8,128)(2,1)} %copy-done.1, bf16[256,128]{1,0:T(8,128)(2,1)} %copy-done.2, bf16[32,256,256]{2,1,0:T(8,128)(2,1)} %lower.9, ...), custom_call_target="tpu_custom_call" | custom-call | flops 536870912 | bytes 5242880 | tf_op jit(solution)/shard_map/op1/pallas_call | solution.py:141
  17.3 1.3 collective-permute-start.2
  18.6 4.7 %op2.1 = bf16[2048,128]{1,0:T(8,128)(2,1)} custom-call(s32[2]{0:T(128)} %pad_add_fusion.meta, bf16[8192,128]{1,0:T(8,128)(2,1)} %nxt.7, bf16[8192,128]{1,0:T(8,128)(2,1)} %nxt.7, bf16[8192,128]{1,0:T(8,128)(2,1)} %nxt.7, bf16[256,128]{1,0:T(8,128)(2,1)} %copy-done.1, bf16[256,128]{1,0:T(8,128)(2,1)} %copy-done.2, bf16[32,256,256]{2,1,0:T(8,128)(2,1)} %lower.9, ...), custom_call_target="tpu_custom_call" | custom-call | flops 536870912 | bytes 5242880 | tf_op jit(solution)/shard_map/op2/pallas_call | solution.py:141
  23.3 2.6 %collective-permute-start.3 = (bf16[2048,128]{1,0:T(8,128)(2,1)}, bf16[2048,128]{1,0:T(8,128)(2,1)S(1)}, u32[]{:S(2)}, u32[]{:S(2)}) collective-permute-start(bf16[2048,128]{1,0:T(8,128)(2,1)} %op2.1), channel_id=1, source_target_pairs={{0,2},{1,3},{2,0},{3,1},{4,6},{5,7},{6,4},{7,5},{8,10},{9,11},{10,... | collective-permute-start | bytes 1572872 | tf_op jit(solution)/shard_map/ppermute | solution.py:59
  25.9 4.7 %op3.1 = bf16[2048,128]{1,0:T(8,128)(2,1)} custom-call(s32[2]{0:T(128)} %pad_add_fusion.meta, bf16[8192,128]{1,0:T(8,128)(2,1)} %nxt.7, bf16[8192,128]{1,0:T(8,128)(2,1)} %nxt.7, bf16[8192,128]{1,0:T(8,128)(2,1)} %nxt.7, bf16[256,128]{1,0:T(8,128)(2,1)} %copy-done.1, bf16[256,128]{1,0:T(8,128)(2,1)} %copy-done.2, bf16[32,256,256]{2,1,0:T(8,128)(2,1)} %lower.9, ...), custom_call_target="tpu_custom_call" | custom-call | flops 536870912 | bytes 5242880 | tf_op jit(solution)/shard_map/op3/pallas_call | solution.py:141
  30.6 1.1 collective-permute-start.4
  31.7 4.7 %op0.1.p0 = bf16[2048,128]{1,0:T(8,128)(2,1)} custom-call(s32[2]{0:T(128)} %pad_add_fusion.meta, bf16[8192,128]{1,0:T(8,128)(2,1)} %nxt.7, bf16[8192,128]{1,0:T(8,128)(2,1)} %nxt.7, bf16[8192,128]{1,0:T(8,128)(2,1)} %nxt.7, bf16[256,128]{1,0:T(8,128)(2,1)} %copy-done.1, bf16[256,128]{1,0:T(8,128)(2,1)} %copy-done.2, bf16[32,256,256]{2,1,0:T(8,128)(2,1)} %lower.9, ...), custom_call_target="tpu_custom_call" | custom-call | flops 536870912 | bytes 5242880 | tf_op jit(solution)/shard_map/op0/pallas_call | solution.py:141
  36.4 6.6 %collective-permute-done.3.p2 = bf16[2048,128]{1,0:T(8,128)(2,1)S(1)} collective-permute-done((bf16[2048,128]{1,0:T(8,128)(2,1)}, bf16[2048,128]{1,0:T(8,128)(2,1)S(1)}, u32[]{:S(2)}, u32[]{:S(2)}) %collective-permute-start.3) | collective-permute-done | bytes 524320 | tf_op jit(solution)/shard_map/ppermute | solution.py:59
  42.9 4.3 %collective-permute-done.4.p3 = bf16[2048,128]{1,0:T(8,128)(2,1)S(1)} collective-permute-done((bf16[2048,128]{1,0:T(8,128)(2,1)}, bf16[2048,128]{1,0:T(8,128)(2,1)S(1)}, u32[]{:S(2)}, u32[]{:S(2)}) %collective-permute-start.4) | collective-permute-done | bytes 524320 | tf_op jit(solution)/shard_map/ppermute | solution.py:59
  47.3 0.8 copy-done.14
  48.0 5.3 %gram.1 = (bf16[2048,512]{1,0:T(8,128)(2,1)}, bf16[256,512]{1,0:T(8,128)(2,1)}, bf16[256,512]{1,0:T(8,128)(2,1)}, f32[640,128]{1,0:T(8,128)}, f32[640,128]{1,0:T(8,128)}) custom-call(s32[2]{0:T(128)} %pad_add_fusion.meta, bf16[2048,128]{1,0:T(8,128)(2,1)} %op0.1.p0, bf16[2048,128]{1,0:T(8,128)(2,1)} %copy-done.12, bf16[2048,128]{1,0:T(8,128)(2,1)} %copy-done.13, ...), custom_call_target="tpu_custom_call" | custom-call | flops 1073741824 | bytes 5242880 | tf_op jit(solution)/shard_map/gram/pallas_call | solution.py:194
  53.3 1.8 %collective-permute-done.5 = f32[640,128]{1,0:T(8,128)S(1)} collective-permute-done((f32[640,128]{1,0:T(8,128)}, f32[640,128]{1,0:T(8,128)S(1)}, u32[]{:S(2)}, u32[]{:S(2)}) %collective-permute-start.5) | collective-permute-done | bytes 327712 | tf_op jit(solution)/shard_map/ppermute | solution.py:48
  55.2 1.7 add.21
  56.9 8.5 %all-to-all-start = ((f32[16,40,128]{2,1,0:T(8,128)}), f32[16,40,128]{2,1,0:T(8,128)S(1)}, u32[]{:S(2)}, u32[]{:S(2)}) async-start(f32[16,40,128]{2,1,0:T(8,128)} %bitcast.2), calls=%async_computation | async-start | bytes 655360 | tf_op jit(solution)/shard_map/all_to_all | solution.py:55
  65.4 4.4 %collective-permute-start.13 = (bf16[256,512]{1,0:T(8,128)(2,1)}, bf16[256,512]{1,0:T(8,128)(2,1)S(1)}, u32[]{:S(2)}, u32[]{:S(2)}) collective-permute-start(bf16[256,512]{1,0:T(8,128)(2,1)} %get-tuple-element.20), channel_id=1, source_target_pairs={{0,1},{1,2},{2,3},{3,4},{4,5},{5,6},{6,7},{7,8},{8,9},{9,10},{10,1... | collective-permute-start | bytes 786440 | tf_op jit(solution)/shard_map/ppermute | solution.py:64
  69.8 2.6 %collective-permute-start.14 = (bf16[256,512]{1,0:T(8,128)(2,1)}, bf16[256,512]{1,0:T(8,128)(2,1)S(1)}, u32[]{:S(2)}, u32[]{:S(2)}) collective-permute-start(bf16[256,512]{1,0:T(8,128)(2,1)} %get-tuple-element.21), channel_id=1, source_target_pairs={{1,0},{2,1},{3,2},{4,3},{5,4},{6,5},{7,6},{8,7},{9,8},{10,9},{11,1... | collective-permute-start | bytes 786440 | tf_op jit(solution)/shard_map/ppermute | solution.py:64
  72.5 1.1 all-to-all-done
  73.6 3.0 %collective-permute-start.6 = (f32[40,128]{1,0:T(8,128)S(1)}, f32[40,128]{1,0:T(8,128)S(1)}, u32[]{:S(2)}, u32[]{:S(2)}) collective-permute-start(f32[40,128]{1,0:T(8,128)S(1)} %reduce_sum.18), channel_id=1, source_target_pairs={{0,2},{1,3},{2,0},{3,1},{4,6},{5,7},{6,4},{7,5},{8,10},{9,11},{10,... | collective-permute-start | bytes 61448 | tf_op jit(solution)/shard_map/ppermute | solution.py:59
  76.7 2.6 %collective-permute-start.8 = (f32[40,128]{1,0:T(8,128)S(1)}, f32[40,128]{1,0:T(8,128)S(1)}, u32[]{:S(2)}, u32[]{:S(2)}) collective-permute-start(f32[40,128]{1,0:T(8,128)S(1)} %reduce_sum.18), channel_id=1, source_target_pairs={{0,3},{1,0},{2,1},{3,2},{4,7},{5,4},{6,5},{7,6},{8,11},{9,8},{10,9... | collective-permute-start | bytes 61448 | tf_op jit(solution)/shard_map/ppermute | solution.py:59
  80.0 8.4 %moment.1 = (f32[256,512]{1,0:T(8,128)}, f32[256,512]{1,0:T(8,128)}) custom-call(s32[2]{0:T(128)} %pad_add_fusion.meta, bf16[2048,512]{1,0:T(8,128)(2,1)} %get-tuple-element.15.wide.prev.cur.nxt, bf16[2048,512]{1,0:T(8,128)(2,1)} %get-tuple-element.15.wide.prev.cur.nxt, bf16[2048,512]{1,0:T(8,128)(2,1)} %get-tuple-element.15.wide.prev.cur.nxt, ...), custom_call_target="tpu_custom_call" | custom-call | flops 3221225472 | bytes 4194304 | tf_op jit(solution)/shard_map/moment/pallas_call | solution.py:249
  88.4 2.8 %collective-permute-start.15 = (f32[256,512]{1,0:T(8,128)}, f32[256,512]{1,0:T(8,128)S(1)}, u32[]{:S(2)}, u32[]{:S(2)}) collective-permute-start(f32[256,512]{1,0:T(8,128)} %get-tuple-element.23), channel_id=1, source_target_pairs={{0,4},{4,0},{8,12},{12,8},{16,20},{20,16},{24,28},{28,24},{32,36},... | collective-permute-start | bytes 1572872 | tf_op jit(solution)/shard_map/ppermute | solution.py:48
  91.2 0.7 broadcast_in_dim.4
  91.9 5.6 %all-to-all-start.1 = ((f32[16,40,128]{2,1,0:T(8,128)}), f32[16,40,128]{2,1,0:T(8,128)S(1)}, u32[]{:S(2)}, u32[]{:S(2)}) async-start(f32[16,40,128]{2,1,0:T(8,128)} %broadcast_in_dim.4), calls=%async_computation.1 | async-start | bytes 655360 | tf_op jit(solution)/shard_map/all_to_all | solution.py:55
  97.6 0.8 copy-done.6
  98.4 2.1 %pack.1 = f32[16,64,128]{2,1,0:T(8,128)} custom-call(f32[256,512]{1,0:T(8,128)} %get-tuple-element.22.keep, f32[256,512]{1,0:T(8,128)} %copy-done.6), custom_call_target="tpu_custom_call" | custom-call | flops 131072 | bytes 1572864 | tf_op jit(solution)/shard_map/pack/pallas_call | solution.py:96
  100.5 5.5 %all-to-all-done.1.mine = f32[16,40,128]{2,1,0:T(8,128)S(1)} async-done(((f32[16,40,128]{2,1,0:T(8,128)}), f32[16,40,128]{2,1,0:T(8,128)S(1)}, u32[]{:S(2)}, u32[]{:S(2)}) %all-to-all-start.1) | async-done | bytes 327712 | tf_op jit(solution)/shard_map/all_to_all | solution.py:55
  105.9 4.0 %all-to-all-start.2 = ((f32[16,64,128]{2,1,0:T(8,128)}), f32[16,64,128]{2,1,0:T(8,128)S(1)}, u32[]{:S(2)}, u32[]{:S(2)}) async-start(f32[16,64,128]{2,1,0:T(8,128)} %pack.1), calls=%async_computation.2 | async-start | bytes 1048576 | tf_op jit(solution)/shard_map/all_to_all | solution.py:55
  110.0 1.5 collective-permute-start.9
  111.5 7.5 %all-to-all-done.2 = f32[16,64,128]{2,1,0:T(8,128)S(1)} async-done(((f32[16,64,128]{2,1,0:T(8,128)}), f32[16,64,128]{2,1,0:T(8,128)S(1)}, u32[]{:S(2)}, u32[]{:S(2)}) %all-to-all-start.2) | async-done | bytes 524320 | tf_op jit(solution)/shard_map/all_to_all | solution.py:55
  119.0 1.4 collective-permute-start.16
  120.4 1.4 collective-permute-start.17
  121.9 1.2 collective-permute-start.18
  123.1 0.7 copy-done.8
  123.8 21.0 %factor.1.linv = bf16[512,512]{1,0:T(8,128)(2,1)} custom-call(s32[2]{0:T(128)} %pad_add_fusion.meta, f32[16,40,128]{2,1,0:T(8,128)} %copy-done, f32[16,40,128]{2,1,0:T(8,128)} %copy-done.8), custom_call_target="tpu_custom_call" | custom-call | flops 134217728 | bytes 3145728 | tf_op jit(solution)/shard_map/factor/pallas_call | solution.py:383
  144.8 5.6 %ortho.1 = (bf16[2048,128]{1,0:T(8,128)(2,1)}, bf16[2048,128]{1,0:T(8,128)(2,1)}, bf16[2048,128]{1,0:T(8,128)(2,1)}, bf16[2048,128]{1,0:T(8,128)(2,1)}) custom-call(s32[2]{0:T(128)} %pad_add_fusion.meta, bf16[512,512]{1,0:T(8,128)(2,1)} %factor.1.linv, bf16[2048,512]{1,0:T(8,128)(2,1)} %get-tuple-element.15.wide.prev.cur.nxt), custom_call_target="tpu_custom_call" | custom-call | flops 1073741824 | bytes 4194304 | tf_op jit(solution)/shard_map/ortho/pallas_call | solution.py:414
  150.7 1.0 collective-permute-start.11
  151.6 1.5 collective-permute-start.12
  153.7 2.6 %tail.1 = f32[16,128]{1,0:T(8,128)} custom-call(s32[2]{0:T(128)} %pad_add_fusion.meta, bf16[512,512]{1,0:T(8,128)(2,1)} %factor.1.linv, f32[64,128]{1,0:T(8,128)} %add_add_fusion.moment), custom_call_target="tpu_custom_call" | custom-call | flops 6291456 | bytes 524288 | tf_op jit(solution)/shard_map/tail/pallas_call | solution.py:470
  157.1 10.8 %all_to_all.20.mine = f32[16,16,128]{2,1,0:T(8,128)S(1)} all-to-all(f32[16,16,128]{2,1,0:T(8,128)S(1)} %broadcast_in_dim.5), channel_id=1, replica_groups={{0,8,16,24,32,40,48,56,64,72,80,88,96,104,112,120},{4,12,20,28,36,44,52..., dimensions={0} | all-to-all | bytes 262144 | tf_op jit(solution)/shard_map/all_to_all | solution.py:55
  167.9 5.3 %collective-permute-start.19 = (f32[16,16,128]{2,1,0:T(8,128)S(1)}, f32[16,16,128]{2,1,0:T(8,128)S(1)}, u32[]{:S(2)}, u32[]{:S(2)}) collective-permute-start(f32[16,16,128]{2,1,0:T(8,128)S(1)} %all_to_all.20.mine), channel_id=1, source_target_pairs={{0,4},{4,0},{8,12},{12,8},{16,20},{20,16},{24,28},{28,24},{32,36},... | collective-permute-start | bytes 393224 | tf_op jit(solution)/shard_map/ppermute | solution.py:48
  173.1 1.0 collective-permute-done.19.other
  174.8 3.1 %project.1 = f32[512,128]{1,0:T(8,128)} custom-call(s32[2]{0:T(128)} %pad_add_fusion.meta, bf16[512,512]{1,0:T(8,128)(2,1)} %factor.1.linv, f32[16,16,128]{2,1,0:T(8,128)} %copy-done.7, f32[16,16,128]{2,1,0:T(8,128)} %copy-done.11), custom_call_target="tpu_custom_call" | custom-call | flops 201326592 | bytes 1048576 | tf_op jit(solution)/shard_map/project/pallas_call | solution.py:492
  177.9 0.8 copy-done.3
  179.1 3.6 %join.1 = bf16[8192,128]{1,0:T(8,128)(2,1)} custom-call(s32[2]{0:T(128)} %pad_add_fusion.meta, bf16[2048,128]{1,0:T(8,128)(2,1)} %get-tuple-element.16.refs_0_, bf16[2048,128]{1,0:T(8,128)(2,1)} %copy-done.3, bf16[2048,128]{1,0:T(8,128)(2,1)} %copy-done.4, bf16[2048,128]{1,0:T(8,128)(2,1)} %copy-done.5), custom_call_target="tpu_custom_call" | custom-call | bytes 4194304 | tf_op jit(solution)/shard_map/join/pallas_call | solution.py:439
  (50 shorter events, 4.9 us)
Async XLA Ops:
  1.5 7.5 %collective-permute-start = (bf16[256,128]{1,0:T(8,128)(2,1)S(1)}, bf16[256,128]{1,0:T(8,128)(2,1)S(1)}, u32[]{:S(2)}, u32[]{:S(2)}) collective-permute-start(bf16[256,128]{1,0:T(8,128)(2,1)S(1)} %get-tuple-element.25), channel_id=1, source_target_pairs={{0,4},{4,8},{8,12},{12,16},{16,20},{20,24},{24,28},{28,32},{32,36}... | collective-permute-start | bytes 196616 | tf_op jit(solution)/shard_map/ppermute | solution.py:514
  6.5 5.6 %collective-permute-start.1 = (bf16[256,128]{1,0:T(8,128)(2,1)S(1)}, bf16[256,128]{1,0:T(8,128)(2,1)S(1)}, u32[]{:S(2)}, u32[]{:S(2)}) collective-permute-start(bf16[256,128]{1,0:T(8,128)(2,1)S(1)} %get-tuple-element.24), channel_id=1, source_target_pairs={{4,0},{8,4},{12,8},{16,12},{20,16},{24,20},{28,24},{32,28},{36,32}... | collective-permute-start | bytes 196616 | tf_op jit(solution)/shard_map/ppermute | solution.py:515
  9.0 3.1 %copy-start.1 = (bf16[256,128]{1,0:T(8,128)(2,1)}, bf16[256,128]{1,0:T(8,128)(2,1)S(1)}, u32[]{:S(2)}) copy-start(bf16[256,128]{1,0:T(8,128)(2,1)S(1)} %collective-permute-done.low) | copy-start | bytes 196612
  12.0 0.6 copy-start.2
  17.3 19.0 %collective-permute-start.2 = (bf16[2048,128]{1,0:T(8,128)(2,1)}, bf16[2048,128]{1,0:T(8,128)(2,1)S(1)}, u32[]{:S(2)}, u32[]{:S(2)}) collective-permute-start(bf16[2048,128]{1,0:T(8,128)(2,1)} %op1.1), channel_id=1, source_target_pairs={{0,1},{1,2},{2,3},{3,0},{4,5},{5,6},{6,7},{7,4},{8,9},{9,10},{10,1... | collective-permute-start | bytes 1572872 | tf_op jit(solution)/shard_map/ppermute | solution.py:59
  23.3 19.6 %collective-permute-start.3 = (bf16[2048,128]{1,0:T(8,128)(2,1)}, bf16[2048,128]{1,0:T(8,128)(2,1)S(1)}, u32[]{:S(2)}, u32[]{:S(2)}) collective-permute-start(bf16[2048,128]{1,0:T(8,128)(2,1)} %op2.1), channel_id=1, source_target_pairs={{0,2},{1,3},{2,0},{3,1},{4,6},{5,7},{6,4},{7,5},{8,10},{9,11},{10,... | collective-permute-start | bytes 1572872 | tf_op jit(solution)/shard_map/ppermute | solution.py:59
  30.6 16.6 %collective-permute-start.4 = (bf16[2048,128]{1,0:T(8,128)(2,1)}, bf16[2048,128]{1,0:T(8,128)(2,1)S(1)}, u32[]{:S(2)}, u32[]{:S(2)}) collective-permute-start(bf16[2048,128]{1,0:T(8,128)(2,1)} %op3.1), channel_id=1, source_target_pairs={{0,3},{1,0},{2,1},{3,2},{4,7},{5,4},{6,5},{7,6},{8,11},{9,8},{10,9... | collective-permute-start | bytes 1572872 | tf_op jit(solution)/shard_map/ppermute | solution.py:59
  36.3 10.9 %copy-start.12 = (bf16[2048,128]{1,0:T(8,128)(2,1)}, bf16[2048,128]{1,0:T(8,128)(2,1)S(1)}, u32[]{:S(2)}) copy-start(bf16[2048,128]{1,0:T(8,128)(2,1)S(1)} %collective-permute-done.2.p1) | copy-start | bytes 1572868
  42.9 4.3 %copy-start.13 = (bf16[2048,128]{1,0:T(8,128)(2,1)}, bf16[2048,128]{1,0:T(8,128)(2,1)S(1)}, u32[]{:S(2)}) copy-start(bf16[2048,128]{1,0:T(8,128)(2,1)S(1)} %collective-permute-done.3.p2) | copy-start | bytes 1572868
  47.2 0.8 copy-start.14
  53.3 1.8 %collective-permute-start.5 = (f32[640,128]{1,0:T(8,128)}, f32[640,128]{1,0:T(8,128)S(1)}, u32[]{:S(2)}, u32[]{:S(2)}) collective-permute-start(f32[640,128]{1,0:T(8,128)} %get-tuple-element.14), channel_id=1, source_target_pairs={{0,4},{4,0},{8,12},{12,8},{16,20},{20,16},{24,28},{28,24},{32,36},... | collective-permute-start | bytes 983048 | tf_op jit(solution)/shard_map/ppermute | solution.py:48
  56.9 16.7 %all-to-all-start = ((f32[16,40,128]{2,1,0:T(8,128)}), f32[16,40,128]{2,1,0:T(8,128)S(1)}, u32[]{:S(2)}, u32[]{:S(2)}) async-start(f32[16,40,128]{2,1,0:T(8,128)} %bitcast.2), calls=%async_computation | async-start | bytes 655360 | tf_op jit(solution)/shard_map/all_to_all | solution.py:55
  65.4 13.9 %collective-permute-start.13 = (bf16[256,512]{1,0:T(8,128)(2,1)}, bf16[256,512]{1,0:T(8,128)(2,1)S(1)}, u32[]{:S(2)}, u32[]{:S(2)}) collective-permute-start(bf16[256,512]{1,0:T(8,128)(2,1)} %get-tuple-element.20), channel_id=1, source_target_pairs={{0,1},{1,2},{2,3},{3,4},{4,5},{5,6},{6,7},{7,8},{8,9},{9,10},{10,1... | collective-permute-start | bytes 786440 | tf_op jit(solution)/shard_map/ppermute | solution.py:64
  69.8 9.4 %collective-permute-start.14 = (bf16[256,512]{1,0:T(8,128)(2,1)}, bf16[256,512]{1,0:T(8,128)(2,1)S(1)}, u32[]{:S(2)}, u32[]{:S(2)}) collective-permute-start(bf16[256,512]{1,0:T(8,128)(2,1)} %get-tuple-element.21), channel_id=1, source_target_pairs={{1,0},{2,1},{3,2},{4,3},{5,4},{6,5},{7,6},{8,7},{9,8},{10,9},{11,1... | collective-permute-start | bytes 786440 | tf_op jit(solution)/shard_map/ppermute | solution.py:64
  73.6 17.6 %collective-permute-start.6 = (f32[40,128]{1,0:T(8,128)S(1)}, f32[40,128]{1,0:T(8,128)S(1)}, u32[]{:S(2)}, u32[]{:S(2)}) collective-permute-start(f32[40,128]{1,0:T(8,128)S(1)} %reduce_sum.18), channel_id=1, source_target_pairs={{0,2},{1,3},{2,0},{3,1},{4,6},{5,7},{6,4},{7,5},{8,10},{9,11},{10,... | collective-permute-start | bytes 61448 | tf_op jit(solution)/shard_map/ppermute | solution.py:59
  76.6 14.6 %collective-permute-start.7 = (f32[40,128]{1,0:T(8,128)S(1)}, f32[40,128]{1,0:T(8,128)S(1)}, u32[]{:S(2)}, u32[]{:S(2)}) collective-permute-start(f32[40,128]{1,0:T(8,128)S(1)} %reduce_sum.18), channel_id=1, source_target_pairs={{0,1},{1,2},{2,3},{3,0},{4,5},{5,6},{6,7},{7,4},{8,9},{9,10},{10,1... | collective-permute-start | bytes 61448 | tf_op jit(solution)/shard_map/ppermute | solution.py:59
  76.7 14.5 %collective-permute-start.8 = (f32[40,128]{1,0:T(8,128)S(1)}, f32[40,128]{1,0:T(8,128)S(1)}, u32[]{:S(2)}, u32[]{:S(2)}) collective-permute-start(f32[40,128]{1,0:T(8,128)S(1)} %reduce_sum.18), channel_id=1, source_target_pairs={{0,3},{1,0},{2,1},{3,2},{4,7},{5,4},{6,5},{7,6},{8,11},{9,8},{10,9... | collective-permute-start | bytes 61448 | tf_op jit(solution)/shard_map/ppermute | solution.py:59
  79.3 0.7 copy-start.9
  79.3 0.8 copy-start.10
  88.4 9.2 %collective-permute-start.15 = (f32[256,512]{1,0:T(8,128)}, f32[256,512]{1,0:T(8,128)S(1)}, u32[]{:S(2)}, u32[]{:S(2)}) collective-permute-start(f32[256,512]{1,0:T(8,128)} %get-tuple-element.23), channel_id=1, source_target_pairs={{0,4},{4,0},{8,12},{12,8},{16,20},{20,16},{24,28},{28,24},{32,36},... | collective-permute-start | bytes 1572872 | tf_op jit(solution)/shard_map/ppermute | solution.py:48
  91.9 14.0 %all-to-all-start.1 = ((f32[16,40,128]{2,1,0:T(8,128)}), f32[16,40,128]{2,1,0:T(8,128)S(1)}, u32[]{:S(2)}, u32[]{:S(2)}) async-start(f32[16,40,128]{2,1,0:T(8,128)} %broadcast_in_dim.4), calls=%async_computation.1 | async-start | bytes 655360 | tf_op jit(solution)/shard_map/all_to_all | solution.py:55
  97.6 0.8 copy-start.6
  105.9 17.2 %copy-start = (f32[16,40,128]{2,1,0:T(8,128)}, f32[16,40,128]{2,1,0:T(8,128)S(1)}, u32[]{:S(2)}) copy-start(f32[16,40,128]{2,1,0:T(8,128)S(1)} %all-to-all-done.1.mine) | copy-start | bytes 983044
  105.9 13.0 %all-to-all-start.2 = ((f32[16,64,128]{2,1,0:T(8,128)}), f32[16,64,128]{2,1,0:T(8,128)S(1)}, u32[]{:S(2)}, u32[]{:S(2)}) async-start(f32[16,64,128]{2,1,0:T(8,128)} %pack.1), calls=%async_computation.2 | async-start | bytes 1048576 | tf_op jit(solution)/shard_map/all_to_all | solution.py:55
  110.0 13.1 %collective-permute-start.9 = (f32[16,40,128]{2,1,0:T(8,128)S(1)}, f32[16,40,128]{2,1,0:T(8,128)S(1)}, u32[]{:S(2)}, u32[]{:S(2)}) collective-permute-start(f32[16,40,128]{2,1,0:T(8,128)S(1)} %all-to-all-done.1.mine), channel_id=1, source_target_pairs={{0,4},{4,0},{8,12},{12,8},{16,20},{20,16},{24,28},{28,24},{32,36},... | collective-permute-start | bytes 983048 | tf_op jit(solution)/shard_map/ppermute | solution.py:48
  119.0 32.6 %collective-permute-start.16 = (f32[64,128]{1,0:T(8,128)S(1)}, f32[64,128]{1,0:T(8,128)S(1)}, u32[]{:S(2)}, u32[]{:S(2)}) collective-permute-start(f32[64,128]{1,0:T(8,128)S(1)} %reduce_sum.19), channel_id=1, source_target_pairs={{0,2},{1,3},{2,0},{3,1},{4,6},{5,7},{6,4},{7,5},{8,10},{9,11},{10,... | collective-permute-start | bytes 98312 | tf_op jit(solution)/shard_map/ppermute | solution.py:59
  120.4 32.7 %collective-permute-start.17 = (f32[64,128]{1,0:T(8,128)S(1)}, f32[64,128]{1,0:T(8,128)S(1)}, u32[]{:S(2)}, u32[]{:S(2)}) collective-permute-start(f32[64,128]{1,0:T(8,128)S(1)} %reduce_sum.19), channel_id=1, source_target_pairs={{0,1},{1,2},{2,3},{3,0},{4,5},{5,6},{6,7},{7,4},{8,9},{9,10},{10,1... | collective-permute-start | bytes 98312 | tf_op jit(solution)/shard_map/ppermute | solution.py:59
  121.9 31.3 %collective-permute-start.18 = (f32[64,128]{1,0:T(8,128)S(1)}, f32[64,128]{1,0:T(8,128)S(1)}, u32[]{:S(2)}, u32[]{:S(2)}) collective-permute-start(f32[64,128]{1,0:T(8,128)S(1)} %reduce_sum.19), channel_id=1, source_target_pairs={{0,3},{1,0},{2,1},{3,2},{4,7},{5,4},{6,5},{7,6},{8,11},{9,8},{10,9... | collective-permute-start | bytes 98312 | tf_op jit(solution)/shard_map/ppermute | solution.py:59
  123.1 0.7 copy-start.8
  150.4 27.5 %collective-permute-start.10 = (bf16[2048,128]{1,0:T(8,128)(2,1)}, bf16[2048,128]{1,0:T(8,128)(2,1)S(1)}, u32[]{:S(2)}, u32[]{:S(2)}) collective-permute-start(bf16[2048,128]{1,0:T(8,128)(2,1)} %get-tuple-element.17), channel_id=1, source_target_pairs={{0,1},{1,2},{2,3},{3,0},{4,5},{5,6},{6,7},{7,4},{8,9},{9,10},{10,1... | collective-permute-start | bytes 1572872 | tf_op jit(solution)/shard_map/ppermute | solution.py:59
  150.7 27.2 %collective-permute-start.11 = (bf16[2048,128]{1,0:T(8,128)(2,1)}, bf16[2048,128]{1,0:T(8,128)(2,1)S(1)}, u32[]{:S(2)}, u32[]{:S(2)}) collective-permute-start(bf16[2048,128]{1,0:T(8,128)(2,1)} %get-tuple-element.18), channel_id=1, source_target_pairs={{0,2},{1,3},{2,0},{3,1},{4,6},{5,7},{6,4},{7,5},{8,10},{9,11},{10,... | collective-permute-start | bytes 1572872 | tf_op jit(solution)/shard_map/ppermute | solution.py:59
  151.6 26.3 %collective-permute-start.12 = (bf16[2048,128]{1,0:T(8,128)(2,1)}, bf16[2048,128]{1,0:T(8,128)(2,1)S(1)}, u32[]{:S(2)}, u32[]{:S(2)}) collective-permute-start(bf16[2048,128]{1,0:T(8,128)(2,1)} %get-tuple-element.19), channel_id=1, source_target_pairs={{0,3},{1,0},{2,1},{3,2},{4,7},{5,4},{6,5},{7,6},{8,11},{9,8},{10,9... | collective-permute-start | bytes 1572872 | tf_op jit(solution)/shard_map/ppermute | solution.py:59
  167.8 6.3 %copy-start.7 = (f32[16,16,128]{2,1,0:T(8,128)}, f32[16,16,128]{2,1,0:T(8,128)S(1)}, u32[]{:S(2)}) copy-start(f32[16,16,128]{2,1,0:T(8,128)S(1)} %all_to_all.20.mine) | copy-start | bytes 393220
  167.9 6.3 %collective-permute-start.19 = (f32[16,16,128]{2,1,0:T(8,128)S(1)}, f32[16,16,128]{2,1,0:T(8,128)S(1)}, u32[]{:S(2)}, u32[]{:S(2)}) collective-permute-start(f32[16,16,128]{2,1,0:T(8,128)S(1)} %all_to_all.20.mine), channel_id=1, source_target_pairs={{0,4},{4,0},{8,12},{12,8},{16,20},{20,16},{24,28},{28,24},{32,36},... | collective-permute-start | bytes 393224 | tf_op jit(solution)/shard_map/ppermute | solution.py:48
  174.1 0.6 copy-start.11
  177.9 0.8 copy-start.3
  177.9 1.0 copy-start.4
  177.9 1.2 copy-start.5
where the time goes:
time: 184 us; the launch traced here: 183 us
  Pallas kernels  70.3 us (38%)
  starting transfers between devices  59 us (32%)
  waiting for transfers between devices  30.9 us (17%)
  blocking collectives  10.8 us (6%)
  local copies, waits for them, and re-layouts  7.87 us (4%)
  other arithmetic  3.03 us (2%)
    pallas_call x1, Pallas kernels, factor_of(): pl.pallas_call(factor_kernel, out_shape=shape((k, k), BF16), grid_spec=pl...  21 us
    pallas_call x4, Pallas kernels, op_chunk(): pl.pallas_call(functools.partial(op_kernel, j=j, per=per, count=count), o...  18.7 us
    all_to_all x3, starting transfers between devices, plane(): lax.all_to_all(value, 'rows', 0, 0, tiled=True, axis_index_groups=PLANE)  18.2 us
    ppermute x12, starting transfers between devices, along_cols(): return lax.ppermute(value, 'cols', [(i, (i + s) % Y) for i in range(Y)])  17.4 us
    all_to_all x3, waiting for transfers between devices, plane(): lax.all_to_all(value, 'rows', 0, 0, tiled=True, axis_index_groups=PLANE)  14.1 us
    ppermute x12, waiting for transfers between devices, along_cols(): return lax.ppermute(value, 'cols', [(i, (i + s) % Y) for i in range(Y)])  10.9 us
    all_to_all x1, blocking collectives, plane(): lax.all_to_all(value, 'rows', 0, 0, tiled=True, axis_index_groups=PLANE)  10.8 us
    ppermute x4, starting transfers between devices, flip(): return lax.ppermute(value, 'rows', over_rows(lambda x, z, c: (x, z, c + 1)))  9.55 us
  transfers between devices with their start and end apart: 23, of which 8 were waited for; matrix products, arithmetic and copies ran while one was open for 1% of the time, Pallas kernels for 31%

commit v1 on v0

--- a/solution.py
+++ b/solution.py
@@ -12,7 +12,8 @@
 HI = lax.Precision.HIGHEST
 X, Z, CORE, Y = 4, 4, 2, 4
 PARTS = 4
-LIMIT = 56 << 20
+LIMIT = 24 << 20
+WHOLE = 56 << 20
 
 
 def dot(a, b, ca=1, cb=0, precision=None):
@@ -160,7 +161,7 @@
             out_specs=pl.BlockSpec((per * size, width), lambda i, m: (i, 0)),
         ),
         cost_estimate=cost(8 * size * size * width * count // Y, 10 * size * size * count // Y),
-        compiler_params=pltpu.CompilerParams(vmem_limit_bytes=LIMIT),
+        compiler_params=pltpu.CompilerParams(vmem_limit_bytes=WHOLE),
         name=f"op{j}",
     )(meta, basis, basis, basis, low, high, lower, diag, upper, inverse)
 
@@ -267,7 +268,7 @@
             scratch_shapes=[pltpu.VMEM((k, k), F32), pltpu.VMEM((per * size, k), BF16)],
         ),
         cost_estimate=cost(blocks * size * k * (8 * size + 2 * k), 4 * blocks * size * k),
-        compiler_params=pltpu.CompilerParams(vmem_limit_bytes=LIMIT),
+        compiler_params=pltpu.CompilerParams(vmem_limit_bytes=WHOLE),
         name="moment",
     )(meta, wide, wide, wide, low, high, lower, diag, upper, inverse)
 

time: 184 us -> 173 us (0.940)
  Pallas kernels: 70.3 us -> 61.4 us
    pallas_call x1, Pallas kernels: 5.28 us -> 2.37 us  [gram_of(): pl.pallas_call(functools.partial(gram_kernel, size=size), out_shape=(shap...]
    pallas_call x1, Pallas kernels: 21 us -> 18.7 us  [factor_of(): pl.pallas_call(factor_kernel, out_shape=shape((k, k), BF16), grid_spec=pl...]
    pallas_call x1, Pallas kernels: 5.62 us -> 3.55 us  [ortho_of(): pl.pallas_call(ortho_kernel, out_shape=[shape((rows, width), BF16)] * Y,...]
    unnamed x30 -> x28, local copies, waits for them, and re-layouts: 5.55 us -> 5.21 us
  transfers between devices with their start and end apart: 23 -> 23, of which waited for: 8 -> 8; matrix products, arithmetic and copies ran while one was open for 1% -> 2% of each run, Pallas kernels for 31% -> 30%
where the time goes in v1:
time: 173 us; the launch traced here: 172 us
  Pallas kernels  61.4 us (35%)
  starting transfers between devices  58.9 us (34%)
  waiting for transfers between devices  30.6 us (18%)
  blocking collectives  10.8 us (6%)
  local copies, waits for them, and re-layouts  7.55 us (4%)
  other arithmetic  2.07 us (1%)
    pallas_call x1, Pallas kernels, factor_of(): pl.pallas_call(factor_kernel, out_shape=shape((k, k), BF16), grid_spec=pl...  18.7 us
    pallas_call x4, Pallas kernels, op_chunk(): pl.pallas_call(functools.partial(op_kernel, j=j, per=per, count=count), o...  18.7 us
    all_to_all x3, starting transfers between devices, plane(): lax.all_to_all(value, 'rows', 0, 0, tiled=True, axis_index_groups=PLANE)  17.9 us
    ppermute x12, starting transfers between devices, along_cols(): return lax.ppermute(value, 'cols', [(i, (i + s) % Y) for i in range(Y)])  17.4 us
    all_to_all x3, waiting for transfers between devices, plane(): lax.all_to_all(value, 'rows', 0, 0, tiled=True, axis_index_groups=PLANE)  14.1 us
    ppermute x12, waiting for transfers between devices, along_cols(): return lax.ppermute(value, 'cols', [(i, (i + s) % Y) for i in range(Y)])  10.9 us
    all_to_all x1, blocking collectives, plane(): lax.all_to_all(value, 'rows', 0, 0, tiled=True, axis_index_groups=PLANE)  10.8 us
    ppermute x4, starting transfers between devices, flip(): return lax.ppermute(value, 'rows', over_rows(lambda x, z, c: (x, z, c + 1)))  9.67 us
  transfers between devices with their start and end apart: 23, of which 8 were waited for; matrix products, arithmetic and copies ran while one was open for 2% of the time, Pallas kernels for 30%

profile of v1, /device:TPU:1, one launch (start us, length us, event | category | flops | bytes accessed | tf_op | source)
XLA Modules:
  0.0 172.2 jit_solution(1828384914834657429)
XLA Ops:
  0.6 0.9 fusion
  1.5 4.9 %collective-permute-start = (bf16[256,128]{1,0:T(8,128)(2,1)S(1)}, bf16[256,128]{1,0:T(8,128)(2,1)S(1)}, u32[]{:S(2)}, u32[]{:S(2)}) collective-permute-start(bf16[256,128]{1,0:T(8,128)(2,1)S(1)} %get-tuple-element.25), channel_id=1, source_target_pairs={{0,4},{4,8},{8,12},{12,16},{16,20},{20,24},{24,28},{28,32},{32,36}... | collective-permute-start | bytes 196616 | tf_op jit(solution)/shard_map/ppermute | solution.py:515
  6.5 1.9 %collective-permute-start.1 = (bf16[256,128]{1,0:T(8,128)(2,1)S(1)}, bf16[256,128]{1,0:T(8,128)(2,1)S(1)}, u32[]{:S(2)}, u32[]{:S(2)}) collective-permute-start(bf16[256,128]{1,0:T(8,128)(2,1)S(1)} %get-tuple-element.24), channel_id=1, source_target_pairs={{4,0},{8,4},{12,8},{16,12},{20,16},{24,20},{28,24},{32,28},{36,32}... | collective-permute-start | bytes 196616 | tf_op jit(solution)/shard_map/ppermute | solution.py:516
  9.0 3.0 %collective-permute-done.1.high = bf16[256,128]{1,0:T(8,128)(2,1)S(1)} collective-permute-done((bf16[256,128]{1,0:T(8,128)(2,1)S(1)}, bf16[256,128]{1,0:T(8,128)(2,1)S(1)}, u32[]{:S(2)}, u32[]{:S(2)}) %collective-permute-start.1) | collective-permute-done | bytes 65568 | tf_op jit(solution)/shard_map/ppermute | solution.py:516
  12.7 4.7 %op1.1 = bf16[2048,128]{1,0:T(8,128)(2,1)} custom-call(s32[2]{0:T(128)} %pad_add_fusion.meta, bf16[8192,128]{1,0:T(8,128)(2,1)} %nxt.7, bf16[8192,128]{1,0:T(8,128)(2,1)} %nxt.7, bf16[8192,128]{1,0:T(8,128)(2,1)} %nxt.7, bf16[256,128]{1,0:T(8,128)(2,1)} %copy-done.7, bf16[256,128]{1,0:T(8,128)(2,1)} %copy-done.8, bf16[32,256,256]{2,1,0:T(8,128)(2,1)} %lower.9, ...), custom_call_target="tpu_custom_call" | custom-call | flops 536870912 | bytes 5242880 | tf_op jit(solution)/shard_map/op1/pallas_call | solution.py:142
  17.3 1.3 collective-permute-start.2
  18.6 4.7 %op2.1 = bf16[2048,128]{1,0:T(8,128)(2,1)} custom-call(s32[2]{0:T(128)} %pad_add_fusion.meta, bf16[8192,128]{1,0:T(8,128)(2,1)} %nxt.7, bf16[8192,128]{1,0:T(8,128)(2,1)} %nxt.7, bf16[8192,128]{1,0:T(8,128)(2,1)} %nxt.7, bf16[256,128]{1,0:T(8,128)(2,1)} %copy-done.7, bf16[256,128]{1,0:T(8,128)(2,1)} %copy-done.8, bf16[32,256,256]{2,1,0:T(8,128)(2,1)} %lower.9, ...), custom_call_target="tpu_custom_call" | custom-call | flops 536870912 | bytes 5242880 | tf_op jit(solution)/shard_map/op2/pallas_call | solution.py:142
  23.3 2.6 %collective-permute-start.3 = (bf16[2048,128]{1,0:T(8,128)(2,1)}, bf16[2048,128]{1,0:T(8,128)(2,1)S(1)}, u32[]{:S(2)}, u32[]{:S(2)}) collective-permute-start(bf16[2048,128]{1,0:T(8,128)(2,1)} %op2.1), channel_id=1, source_target_pairs={{0,2},{1,3},{2,0},{3,1},{4,6},{5,7},{6,4},{7,5},{8,10},{9,11},{10,... | collective-permute-start | bytes 1572872 | tf_op jit(solution)/shard_map/ppermute | solution.py:60
  25.9 4.7 %op3.1 = bf16[2048,128]{1,0:T(8,128)(2,1)} custom-call(s32[2]{0:T(128)} %pad_add_fusion.meta, bf16[8192,128]{1,0:T(8,128)(2,1)} %nxt.7, bf16[8192,128]{1,0:T(8,128)(2,1)} %nxt.7, bf16[8192,128]{1,0:T(8,128)(2,1)} %nxt.7, bf16[256,128]{1,0:T(8,128)(2,1)} %copy-done.7, bf16[256,128]{1,0:T(8,128)(2,1)} %copy-done.8, bf16[32,256,256]{2,1,0:T(8,128)(2,1)} %lower.9, ...), custom_call_target="tpu_custom_call" | custom-call | flops 536870912 | bytes 5242880 | tf_op jit(solution)/shard_map/op3/pallas_call | solution.py:142
  30.6 1.1 collective-permute-start.4
  31.7 4.7 %op0.1.p0 = bf16[2048,128]{1,0:T(8,128)(2,1)} custom-call(s32[2]{0:T(128)} %pad_add_fusion.meta, bf16[8192,128]{1,0:T(8,128)(2,1)} %nxt.7, bf16[8192,128]{1,0:T(8,128)(2,1)} %nxt.7, bf16[8192,128]{1,0:T(8,128)(2,1)} %nxt.7, bf16[256,128]{1,0:T(8,128)(2,1)} %copy-done.7, bf16[256,128]{1,0:T(8,128)(2,1)} %copy-done.8, bf16[32,256,256]{2,1,0:T(8,128)(2,1)} %lower.9, ...), custom_call_target="tpu_custom_call" | custom-call | flops 536870912 | bytes 5242880 | tf_op jit(solution)/shard_map/op0/pallas_call | solution.py:142
  36.4 6.5 %collective-permute-done.3.p2 = bf16[2048,128]{1,0:T(8,128)(2,1)S(1)} collective-permute-done((bf16[2048,128]{1,0:T(8,128)(2,1)}, bf16[2048,128]{1,0:T(8,128)(2,1)S(1)}, u32[]{:S(2)}, u32[]{:S(2)}) %collective-permute-start.3) | collective-permute-done | bytes 524320 | tf_op jit(solution)/shard_map/ppermute | solution.py:60
  42.9 4.3 %collective-permute-done.4.p3 = bf16[2048,128]{1,0:T(8,128)(2,1)S(1)} collective-permute-done((bf16[2048,128]{1,0:T(8,128)(2,1)}, bf16[2048,128]{1,0:T(8,128)(2,1)S(1)}, u32[]{:S(2)}, u32[]{:S(2)}) %collective-permute-start.4) | collective-permute-done | bytes 524320 | tf_op jit(solution)/shard_map/ppermute | solution.py:60
  47.3 1.0 copy-done.3
  48.3 2.4 %gram.1 = (bf16[2048,512]{1,0:T(8,128)(2,1)S(1)}, bf16[256,512]{1,0:T(8,128)(2,1)S(1)}, bf16[256,512]{1,0:T(8,128)(2,1)S(1)}, f32[640,128]{1,0:T(8,128)S(1)}, f32[640,128]{1,0:T(8,128)S(1)}) custom-call(s32[2]{0:T(128)S(1)} %copy-done.4, bf16[2048,128]{1,0:T(8,128)(2,1)S(1)} %copy-done.3, bf16[2048,128]{1,0:T(8,128)(2,1)S(1)} %collective-permute-done.2.p1, ...), custom_call_target="tpu_custom_call" | custom-call | flops 1073741824 | bytes 5242880 | tf_op jit(solution)/shard_map/gram/pallas_call | solution.py:195
  50.7 1.3 copy-done
  52.0 1.6 collective-permute-done.5
  53.6 0.8 add.21
  54.4 8.5 %all-to-all-start = ((f32[16,40,128]{2,1,0:T(8,128)}), f32[16,40,128]{2,1,0:T(8,128)S(1)}, u32[]{:S(2)}, u32[]{:S(2)}) async-start(f32[16,40,128]{2,1,0:T(8,128)} %bitcast.2), calls=%async_computation | async-start | bytes 655360 | tf_op jit(solution)/shard_map/all_to_all | solution.py:56
  62.9 4.5 %collective-permute-start.13 = (bf16[256,512]{1,0:T(8,128)(2,1)S(1)}, bf16[256,512]{1,0:T(8,128)(2,1)S(1)}, u32[]{:S(2)}, u32[]{:S(2)}) collective-permute-start(bf16[256,512]{1,0:T(8,128)(2,1)S(1)} %get-tuple-element.20), channel_id=1, source_target_pairs={{0,1},{1,2},{2,3},{3,4},{4,5},{5,6},{6,7},{7,8},{8,9},{9,10},{10,1... | collective-permute-start | bytes 786440 | tf_op jit(solution)/shard_map/ppermute | solution.py:65
  67.3 2.6 %collective-permute-start.14 = (bf16[256,512]{1,0:T(8,128)(2,1)S(1)}, bf16[256,512]{1,0:T(8,128)(2,1)S(1)}, u32[]{:S(2)}, u32[]{:S(2)}) collective-permute-start(bf16[256,512]{1,0:T(8,128)(2,1)S(1)} %get-tuple-element.21), channel_id=1, source_target_pairs={{1,0},{2,1},{3,2},{4,3},{5,4},{6,5},{7,6},{8,7},{9,8},{10,9},{11,1... | collective-permute-start | bytes 786440 | tf_op jit(solution)/shard_map/ppermute | solution.py:65
  69.9 1.1 all-to-all-done
  71.1 3.0 %collective-permute-start.6 = (f32[40,128]{1,0:T(8,128)S(1)}, f32[40,128]{1,0:T(8,128)S(1)}, u32[]{:S(2)}, u32[]{:S(2)}) collective-permute-start(f32[40,128]{1,0:T(8,128)S(1)} %reduce_sum.18), channel_id=1, source_target_pairs={{0,2},{1,3},{2,0},{3,1},{4,6},{5,7},{6,4},{7,5},{8,10},{9,11},{10,... | collective-permute-start | bytes 61448 | tf_op jit(solution)/shard_map/ppermute | solution.py:60
  74.1 2.6 %collective-permute-start.8 = (f32[40,128]{1,0:T(8,128)S(1)}, f32[40,128]{1,0:T(8,128)S(1)}, u32[]{:S(2)}, u32[]{:S(2)}) collective-permute-start(f32[40,128]{1,0:T(8,128)S(1)} %reduce_sum.18), channel_id=1, source_target_pairs={{0,3},{1,0},{2,1},{3,2},{4,7},{5,4},{6,5},{7,6},{8,11},{9,8},{10,9... | collective-permute-start | bytes 61448 | tf_op jit(solution)/shard_map/ppermute | solution.py:60
  77.5 8.3 %moment.1 = (f32[256,512]{1,0:T(8,128)}, f32[256,512]{1,0:T(8,128)}) custom-call(s32[2]{0:T(128)} %pad_add_fusion.meta, bf16[2048,512]{1,0:T(8,128)(2,1)} %copy-done, bf16[2048,512]{1,0:T(8,128)(2,1)} %copy-done, bf16[2048,512]{1,0:T(8,128)(2,1)} %copy-done, bf16[256,512]{1,0:T(8,128)(2,1)} %copy-done.11, bf16[256,512]{1,0:T(8,128)(2,1)} %copy-done.12, ...), custom_call_target="tpu_custom_call" | custom-call | flops 3221225472 | bytes 4194304 | tf_op jit(solution)/shard_map/moment/pallas_call | solution.py:250
  85.9 2.9 %collective-permute-start.15 = (f32[256,512]{1,0:T(8,128)}, f32[256,512]{1,0:T(8,128)S(1)}, u32[]{:S(2)}, u32[]{:S(2)}) collective-permute-start(f32[256,512]{1,0:T(8,128)} %get-tuple-element.23), channel_id=1, source_target_pairs={{0,4},{4,0},{8,12},{12,8},{16,20},{20,16},{24,28},{28,24},{32,36},... | collective-permute-start | bytes 1572872 | tf_op jit(solution)/shard_map/ppermute | solution.py:49
  88.7 0.8 broadcast_in_dim.4
  89.5 5.4 %all-to-all-start.1 = ((f32[16,40,128]{2,1,0:T(8,128)}), f32[16,40,128]{2,1,0:T(8,128)S(1)}, u32[]{:S(2)}, u32[]{:S(2)}) async-start(f32[16,40,128]{2,1,0:T(8,128)} %broadcast_in_dim.4), calls=%async_computation.1 | async-start | bytes 655360 | tf_op jit(solution)/shard_map/all_to_all | solution.py:56
  95.0 0.8 copy-done.9
  95.8 2.1 %pack.1 = f32[16,64,128]{2,1,0:T(8,128)} custom-call(f32[256,512]{1,0:T(8,128)} %get-tuple-element.22.keep, f32[256,512]{1,0:T(8,128)} %copy-done.9), custom_call_target="tpu_custom_call" | custom-call | flops 131072 | bytes 1572864 | tf_op jit(solution)/shard_map/pack/pallas_call | solution.py:97
  97.8 5.5 %all-to-all-done.1.mine = f32[16,40,128]{2,1,0:T(8,128)S(1)} async-done(((f32[16,40,128]{2,1,0:T(8,128)}), f32[16,40,128]{2,1,0:T(8,128)S(1)}, u32[]{:S(2)}, u32[]{:S(2)}) %all-to-all-start.1) | async-done | bytes 327712 | tf_op jit(solution)/shard_map/all_to_all | solution.py:56
  103.3 4.0 %all-to-all-start.2 = ((f32[16,64,128]{2,1,0:T(8,128)}), f32[16,64,128]{2,1,0:T(8,128)S(1)}, u32[]{:S(2)}, u32[]{:S(2)}) async-start(f32[16,64,128]{2,1,0:T(8,128)} %pack.1), calls=%async_computation.2 | async-start | bytes 1048576 | tf_op jit(solution)/shard_map/all_to_all | solution.py:56
  107.3 1.5 collective-permute-start.9
  108.8 7.5 %all-to-all-done.2 = f32[16,64,128]{2,1,0:T(8,128)S(1)} async-done(((f32[16,64,128]{2,1,0:T(8,128)}), f32[16,64,128]{2,1,0:T(8,128)S(1)}, u32[]{:S(2)}, u32[]{:S(2)}) %all-to-all-start.2) | async-done | bytes 524320 | tf_op jit(solution)/shard_map/all_to_all | solution.py:56
  116.4 1.4 collective-permute-start.16
  117.7 1.5 collective-permute-start.17
  119.2 1.2 collective-permute-start.18
  120.4 18.7 %factor.1.linv = bf16[512,512]{1,0:T(8,128)(2,1)S(1)} custom-call(s32[2]{0:T(128)S(1)} %copy-done.5, f32[16,40,128]{2,1,0:T(8,128)S(1)} %all-to-all-done.1.mine, f32[16,40,128]{2,1,0:T(8,128)S(1)} %collective-permute-done.9.other), custom_call_target="tpu_custom_call" | custom-call | flops 134217728 | bytes 3145728 | tf_op jit(solution)/shard_map/factor/pallas_call | solution.py:384
  139.2 3.6 %ortho.1 = (bf16[2048,128]{1,0:T(8,128)(2,1)S(1)}, bf16[2048,128]{1,0:T(8,128)(2,1)}, bf16[2048,128]{1,0:T(8,128)(2,1)}, bf16[2048,128]{1,0:T(8,128)(2,1)}) custom-call(s32[2]{0:T(128)S(1)} %copy-done.5, bf16[512,512]{1,0:T(8,128)(2,1)S(1)} %factor.1.linv, bf16[2048,512]{1,0:T(8,128)(2,1)S(1)} %copy-done.1), custom_call_target="tpu_custom_call" | custom-call | flops 1073741824 | bytes 4194304 | tf_op jit(solution)/shard_map/ortho/pallas_call | solution.py:415
  143.0 1.0 collective-permute-start.11
  144.0 1.5 collective-permute-start.12
  146.1 2.6 %tail.1 = f32[16,128]{1,0:T(8,128)} custom-call(s32[2]{0:T(128)} %pad_add_fusion.meta, bf16[512,512]{1,0:T(8,128)(2,1)} %copy-done.2, f32[64,128]{1,0:T(8,128)} %add_add_fusion.moment), custom_call_target="tpu_custom_call" | custom-call | flops 6291456 | bytes 524288 | tf_op jit(solution)/shard_map/tail/pallas_call | solution.py:471
  148.7 0.7 broadcast_in_dim.5
  149.4 10.8 %all_to_all.20.mine = f32[16,16,128]{2,1,0:T(8,128)S(1)} all-to-all(f32[16,16,128]{2,1,0:T(8,128)S(1)} %broadcast_in_dim.5), channel_id=1, replica_groups={{0,8,16,24,32,40,48,56,64,72,80,88,96,104,112,120},{4,12,20,28,36,44,52..., dimensions={0} | all-to-all | bytes 262144 | tf_op jit(solution)/shard_map/all_to_all | solution.py:56
  160.2 5.3 %collective-permute-start.19 = (f32[16,16,128]{2,1,0:T(8,128)S(1)}, f32[16,16,128]{2,1,0:T(8,128)S(1)}, u32[]{:S(2)}, u32[]{:S(2)}) collective-permute-start(f32[16,16,128]{2,1,0:T(8,128)S(1)} %all_to_all.20.mine), channel_id=1, source_target_pairs={{0,4},{4,0},{8,12},{12,8},{16,20},{20,16},{24,28},{28,24},{32,36},... | collective-permute-start | bytes 393224 | tf_op jit(solution)/shard_map/ppermute | solution.py:49
  165.5 1.0 collective-permute-done.19.other
  167.1 3.1 %project.1 = f32[512,128]{1,0:T(8,128)} custom-call(s32[2]{0:T(128)} %pad_add_fusion.meta, bf16[512,512]{1,0:T(8,128)(2,1)} %copy-done.2, f32[16,16,128]{2,1,0:T(8,128)} %copy-done.10, f32[16,16,128]{2,1,0:T(8,128)} %copy-done.13), custom_call_target="tpu_custom_call" | custom-call | flops 201326592 | bytes 1048576 | tf_op jit(solution)/shard_map/project/pallas_call | solution.py:493
  170.2 2.0 %join.1 = bf16[8192,128]{1,0:T(8,128)(2,1)} custom-call(s32[2]{0:T(128)S(1)} %copy-done.6, bf16[2048,128]{1,0:T(8,128)(2,1)S(1)} %get-tuple-element.16.refs_0_, bf16[2048,128]{1,0:T(8,128)(2,1)S(1)} %collective-permute-done.10.refs_1_, bf16[2048,128]{1,0:T(8,128)(2,1)S(1)} %collective-permute-done.11.refs_2_, ...), custom_call_target="tpu_custom_call" | custom-call | bytes 4194304 | tf_op jit(solution)/shard_map/join/pallas_call | solution.py:440
  (48 shorter events, 3.8 us)
Async XLA Ops:
  1.5 7.5 %collective-permute-start = (bf16[256,128]{1,0:T(8,128)(2,1)S(1)}, bf16[256,128]{1,0:T(8,128)(2,1)S(1)}, u32[]{:S(2)}, u32[]{:S(2)}) collective-permute-start(bf16[256,128]{1,0:T(8,128)(2,1)S(1)} %get-tuple-element.25), channel_id=1, source_target_pairs={{0,4},{4,8},{8,12},{12,16},{16,20},{20,24},{24,28},{28,32},{32,36}... | collective-permute-start | bytes 196616 | tf_op jit(solution)/shard_map/ppermute | solution.py:515
  6.5 5.6 %collective-permute-start.1 = (bf16[256,128]{1,0:T(8,128)(2,1)S(1)}, bf16[256,128]{1,0:T(8,128)(2,1)S(1)}, u32[]{:S(2)}, u32[]{:S(2)}) collective-permute-start(bf16[256,128]{1,0:T(8,128)(2,1)S(1)} %get-tuple-element.24), channel_id=1, source_target_pairs={{4,0},{8,4},{12,8},{16,12},{20,16},{24,20},{28,24},{32,28},{36,32}... | collective-permute-start | bytes 196616 | tf_op jit(solution)/shard_map/ppermute | solution.py:516
  9.0 3.0 %copy-start.7 = (bf16[256,128]{1,0:T(8,128)(2,1)}, bf16[256,128]{1,0:T(8,128)(2,1)S(1)}, u32[]{:S(2)}) copy-start(bf16[256,128]{1,0:T(8,128)(2,1)S(1)} %collective-permute-done.low) | copy-start | bytes 196612
  12.0 0.6 copy-start.8
  17.3 19.1 %collective-permute-start.2 = (bf16[2048,128]{1,0:T(8,128)(2,1)}, bf16[2048,128]{1,0:T(8,128)(2,1)S(1)}, u32[]{:S(2)}, u32[]{:S(2)}) collective-permute-start(bf16[2048,128]{1,0:T(8,128)(2,1)} %op1.1), channel_id=1, source_target_pairs={{0,1},{1,2},{2,3},{3,0},{4,5},{5,6},{6,7},{7,4},{8,9},{9,10},{10,1... | collective-permute-start | bytes 1572872 | tf_op jit(solution)/shard_map/ppermute | solution.py:60
  23.3 19.6 %collective-permute-start.3 = (bf16[2048,128]{1,0:T(8,128)(2,1)}, bf16[2048,128]{1,0:T(8,128)(2,1)S(1)}, u32[]{:S(2)}, u32[]{:S(2)}) collective-permute-start(bf16[2048,128]{1,0:T(8,128)(2,1)} %op2.1), channel_id=1, source_target_pairs={{0,2},{1,3},{2,0},{3,1},{4,6},{5,7},{6,4},{7,5},{8,10},{9,11},{10,... | collective-permute-start | bytes 1572872 | tf_op jit(solution)/shard_map/ppermute | solution.py:60
  30.6 16.7 %copy-start.4 = (s32[2]{0:T(128)S(1)}, s32[2]{0:T(128)}, u32[]{:S(2)}) copy-start(s32[2]{0:T(128)} %pad_add_fusion.meta) | copy-start | bytes 28
  30.6 16.7 %collective-permute-start.4 = (bf16[2048,128]{1,0:T(8,128)(2,1)}, bf16[2048,128]{1,0:T(8,128)(2,1)S(1)}, u32[]{:S(2)}, u32[]{:S(2)}) collective-permute-start(bf16[2048,128]{1,0:T(8,128)(2,1)} %op3.1), channel_id=1, source_target_pairs={{0,3},{1,0},{2,1},{3,2},{4,7},{5,4},{6,5},{7,6},{8,11},{9,8},{10,9... | collective-permute-start | bytes 1572872 | tf_op jit(solution)/shard_map/ppermute | solution.py:60
  47.3 1.0 copy-start.3
  50.7 1.3 copy-start
  52.0 1.6 collective-permute-start.5
  54.4 16.7 %all-to-all-start = ((f32[16,40,128]{2,1,0:T(8,128)}), f32[16,40,128]{2,1,0:T(8,128)S(1)}, u32[]{:S(2)}, u32[]{:S(2)}) async-start(f32[16,40,128]{2,1,0:T(8,128)} %bitcast.2), calls=%async_computation | async-start | bytes 655360 | tf_op jit(solution)/shard_map/all_to_all | solution.py:56
  62.9 13.9 %collective-permute-start.13 = (bf16[256,512]{1,0:T(8,128)(2,1)S(1)}, bf16[256,512]{1,0:T(8,128)(2,1)S(1)}, u32[]{:S(2)}, u32[]{:S(2)}) collective-permute-start(bf16[256,512]{1,0:T(8,128)(2,1)S(1)} %get-tuple-element.20), channel_id=1, source_target_pairs={{0,1},{1,2},{2,3},{3,4},{4,5},{5,6},{6,7},{7,8},{8,9},{9,10},{10,1... | collective-permute-start | bytes 786440 | tf_op jit(solution)/shard_map/ppermute | solution.py:65
  67.3 9.4 %collective-permute-start.14 = (bf16[256,512]{1,0:T(8,128)(2,1)S(1)}, bf16[256,512]{1,0:T(8,128)(2,1)S(1)}, u32[]{:S(2)}, u32[]{:S(2)}) collective-permute-start(bf16[256,512]{1,0:T(8,128)(2,1)S(1)} %get-tuple-element.21), channel_id=1, source_target_pairs={{1,0},{2,1},{3,2},{4,3},{5,4},{6,5},{7,6},{8,7},{9,8},{10,9},{11,1... | collective-permute-start | bytes 786440 | tf_op jit(solution)/shard_map/ppermute | solution.py:65
  71.1 17.6 %collective-permute-start.6 = (f32[40,128]{1,0:T(8,128)S(1)}, f32[40,128]{1,0:T(8,128)S(1)}, u32[]{:S(2)}, u32[]{:S(2)}) collective-permute-start(f32[40,128]{1,0:T(8,128)S(1)} %reduce_sum.18), channel_id=1, source_target_pairs={{0,2},{1,3},{2,0},{3,1},{4,6},{5,7},{6,4},{7,5},{8,10},{9,11},{10,... | collective-permute-start | bytes 61448 | tf_op jit(solution)/shard_map/ppermute | solution.py:60
  74.1 14.7 %collective-permute-start.7 = (f32[40,128]{1,0:T(8,128)S(1)}, f32[40,128]{1,0:T(8,128)S(1)}, u32[]{:S(2)}, u32[]{:S(2)}) collective-permute-start(f32[40,128]{1,0:T(8,128)S(1)} %reduce_sum.18), channel_id=1, source_target_pairs={{0,1},{1,2},{2,3},{3,0},{4,5},{5,6},{6,7},{7,4},{8,9},{9,10},{10,1... | collective-permute-start | bytes 61448 | tf_op jit(solution)/shard_map/ppermute | solution.py:60
  74.1 14.6 %collective-permute-start.8 = (f32[40,128]{1,0:T(8,128)S(1)}, f32[40,128]{1,0:T(8,128)S(1)}, u32[]{:S(2)}, u32[]{:S(2)}) collective-permute-start(f32[40,128]{1,0:T(8,128)S(1)} %reduce_sum.18), channel_id=1, source_target_pairs={{0,3},{1,0},{2,1},{3,2},{4,7},{5,4},{6,5},{7,6},{8,11},{9,8},{10,9... | collective-permute-start | bytes 61448 | tf_op jit(solution)/shard_map/ppermute | solution.py:60
  76.7 0.7 copy-start.11
  76.7 0.8 copy-start.12
  85.9 34.6 %copy-start.5 = (s32[2]{0:T(128)S(1)}, s32[2]{0:T(128)}, u32[]{:S(2)}) copy-start(s32[2]{0:T(128)} %pad_add_fusion.meta) | copy-start | bytes 28
  85.9 53.3 %copy-start.1 = (bf16[2048,512]{1,0:T(8,128)(2,1)S(1)}, bf16[2048,512]{1,0:T(8,128)(2,1)}, u32[]{:S(2)}) copy-start(bf16[2048,512]{1,0:T(8,128)(2,1)} %copy-done) | copy-start | bytes 6291460
  85.9 9.1 %collective-permute-start.15 = (f32[256,512]{1,0:T(8,128)}, f32[256,512]{1,0:T(8,128)S(1)}, u32[]{:S(2)}, u32[]{:S(2)}) collective-permute-start(f32[256,512]{1,0:T(8,128)} %get-tuple-element.23), channel_id=1, source_target_pairs={{0,4},{4,0},{8,12},{12,8},{16,20},{20,16},{24,28},{28,24},{32,36},... | collective-permute-start | bytes 1572872 | tf_op jit(solution)/shard_map/ppermute | solution.py:49
  89.5 13.8 %all-to-all-start.1 = ((f32[16,40,128]{2,1,0:T(8,128)}), f32[16,40,128]{2,1,0:T(8,128)S(1)}, u32[]{:S(2)}, u32[]{:S(2)}) async-start(f32[16,40,128]{2,1,0:T(8,128)} %broadcast_in_dim.4), calls=%async_computation.1 | async-start | bytes 655360 | tf_op jit(solution)/shard_map/all_to_all | solution.py:56
  95.0 0.8 copy-start.9
  103.3 13.1 %all-to-all-start.2 = ((f32[16,64,128]{2,1,0:T(8,128)}), f32[16,64,128]{2,1,0:T(8,128)S(1)}, u32[]{:S(2)}, u32[]{:S(2)}) async-start(f32[16,64,128]{2,1,0:T(8,128)} %pack.1), calls=%async_computation.2 | async-start | bytes 1048576 | tf_op jit(solution)/shard_map/all_to_all | solution.py:56
  107.3 62.9 %copy-start.6 = (s32[2]{0:T(128)S(1)}, s32[2]{0:T(128)}, u32[]{:S(2)}) copy-start(s32[2]{0:T(128)} %pad_add_fusion.meta) | copy-start | bytes 28
  107.3 13.1 %collective-permute-start.9 = (f32[16,40,128]{2,1,0:T(8,128)S(1)}, f32[16,40,128]{2,1,0:T(8,128)S(1)}, u32[]{:S(2)}, u32[]{:S(2)}) collective-permute-start(f32[16,40,128]{2,1,0:T(8,128)S(1)} %all-to-all-done.1.mine), channel_id=1, source_target_pairs={{0,4},{4,0},{8,12},{12,8},{16,20},{20,16},{24,28},{28,24},{32,36},... | collective-permute-start | bytes 983048 | tf_op jit(solution)/shard_map/ppermute | solution.py:49
  116.4 27.6 %collective-permute-start.16 = (f32[64,128]{1,0:T(8,128)S(1)}, f32[64,128]{1,0:T(8,128)S(1)}, u32[]{:S(2)}, u32[]{:S(2)}) collective-permute-start(f32[64,128]{1,0:T(8,128)S(1)} %reduce_sum.19), channel_id=1, source_target_pairs={{0,2},{1,3},{2,0},{3,1},{4,6},{5,7},{6,4},{7,5},{8,10},{9,11},{10,... | collective-permute-start | bytes 98312 | tf_op jit(solution)/shard_map/ppermute | solution.py:60
  117.7 27.7 %collective-permute-start.17 = (f32[64,128]{1,0:T(8,128)S(1)}, f32[64,128]{1,0:T(8,128)S(1)}, u32[]{:S(2)}, u32[]{:S(2)}) collective-permute-start(f32[64,128]{1,0:T(8,128)S(1)} %reduce_sum.19), channel_id=1, source_target_pairs={{0,1},{1,2},{2,3},{3,0},{4,5},{5,6},{6,7},{7,4},{8,9},{9,10},{10,1... | collective-permute-start | bytes 98312 | tf_op jit(solution)/shard_map/ppermute | solution.py:60
  119.2 26.2 %collective-permute-start.18 = (f32[64,128]{1,0:T(8,128)S(1)}, f32[64,128]{1,0:T(8,128)S(1)}, u32[]{:S(2)}, u32[]{:S(2)}) collective-permute-start(f32[64,128]{1,0:T(8,128)S(1)} %reduce_sum.19), channel_id=1, source_target_pairs={{0,3},{1,0},{2,1},{3,2},{4,7},{5,4},{6,5},{7,6},{8,11},{9,8},{10,9... | collective-permute-start | bytes 98312 | tf_op jit(solution)/shard_map/ppermute | solution.py:60
  139.2 6.9 %copy-start.2 = (bf16[512,512]{1,0:T(8,128)(2,1)}, bf16[512,512]{1,0:T(8,128)(2,1)S(1)}, u32[]{:S(2)}) copy-start(bf16[512,512]{1,0:T(8,128)(2,1)S(1)} %factor.1.linv) | copy-start | bytes 1572868
  142.7 27.5 %collective-permute-start.10 = (bf16[2048,128]{1,0:T(8,128)(2,1)}, bf16[2048,128]{1,0:T(8,128)(2,1)S(1)}, u32[]{:S(2)}, u32[]{:S(2)}) collective-permute-start(bf16[2048,128]{1,0:T(8,128)(2,1)} %get-tuple-element.17), channel_id=1, source_target_pairs={{0,1},{1,2},{2,3},{3,0},{4,5},{5,6},{6,7},{7,4},{8,9},{9,10},{10,1... | collective-permute-start | bytes 1572872 | tf_op jit(solution)/shard_map/ppermute | solution.py:60
  143.0 27.2 %collective-permute-start.11 = (bf16[2048,128]{1,0:T(8,128)(2,1)}, bf16[2048,128]{1,0:T(8,128)(2,1)S(1)}, u32[]{:S(2)}, u32[]{:S(2)}) collective-permute-start(bf16[2048,128]{1,0:T(8,128)(2,1)} %get-tuple-element.18), channel_id=1, source_target_pairs={{0,2},{1,3},{2,0},{3,1},{4,6},{5,7},{6,4},{7,5},{8,10},{9,11},{10,... | collective-permute-start | bytes 1572872 | tf_op jit(solution)/shard_map/ppermute | solution.py:60
  144.0 26.3 %collective-permute-start.12 = (bf16[2048,128]{1,0:T(8,128)(2,1)}, bf16[2048,128]{1,0:T(8,128)(2,1)S(1)}, u32[]{:S(2)}, u32[]{:S(2)}) collective-permute-start(bf16[2048,128]{1,0:T(8,128)(2,1)} %get-tuple-element.19), channel_id=1, source_target_pairs={{0,3},{1,0},{2,1},{3,2},{4,7},{5,4},{6,5},{7,6},{8,11},{9,8},{10,9... | collective-permute-start | bytes 1572872 | tf_op jit(solution)/shard_map/ppermute | solution.py:60
  160.2 6.3 %copy-start.10 = (f32[16,16,128]{2,1,0:T(8,128)}, f32[16,16,128]{2,1,0:T(8,128)S(1)}, u32[]{:S(2)}) copy-start(f32[16,16,128]{2,1,0:T(8,128)S(1)} %all_to_all.20.mine) | copy-start | bytes 393220
  160.2 6.3 %collective-permute-start.19 = (f32[16,16,128]{2,1,0:T(8,128)S(1)}, f32[16,16,128]{2,1,0:T(8,128)S(1)}, u32[]{:S(2)}, u32[]{:S(2)}) collective-permute-start(f32[16,16,128]{2,1,0:T(8,128)S(1)} %all_to_all.20.mine), channel_id=1, source_target_pairs={{0,4},{4,0},{8,12},{12,8},{16,20},{20,16},{24,28},{28,24},{32,36},... | collective-permute-start | bytes 393224 | tf_op jit(solution)/shard_map/ppermute | solution.py:49
  166.5 0.6 copy-start.13

commit v2 on v1

--- a/solution.py
+++ b/solution.py
@@ -70,7 +70,7 @@
 
 
 def total_of(pieces):
-    total = jnp.sum(plane(pieces), axis=0)
+    total = jnp.sum(plane(pieces).astype(F32), axis=0)
     r1, r2, r3 = (along_cols(total, s) for s in (1, 2, 3))
     return (total + r2) + (r1 + r3)
 
@@ -88,7 +88,7 @@
             at = slice(d * width, (d + 1) * width)
             out[p, d * q : (d + 1) * q, :] = (
                 keep[p * q : (p + 1) * q, at] + got[p * q : (p + 1) * q, at]
-            )
+            ).astype(out.dtype)
 
 
 def pack(keep, got):
@@ -96,7 +96,7 @@
     width = keep.shape[1] // Y
     return pl.pallas_call(
         pack_kernel,
-        out_shape=shape((groups, keep.shape[0] * Y // groups, width), F32),
+        out_shape=shape((groups, keep.shape[0] * Y // groups, width), BF16),
         in_specs=[vmem()] * 2,
         out_specs=vmem(),
         cost_estimate=cost(keep.size, 12 * keep.size),

time: 173 us -> 171 us (0.988)
  transfers between devices with their start and end apart: 23 -> 23, of which waited for: 8 -> 8; matrix products, arithmetic and copies ran while one was open for 2% -> 2% of each run, Pallas kernels for 30% -> 31%
where the time goes in v2:
time: 171 us; the launch traced here: 170 us
  Pallas kernels  61.5 us (36%)
  starting transfers between devices  59 us (35%)
  waiting for transfers between devices  29.1 us (17%)
  blocking collectives  10.1 us (6%)
  local copies, waits for them, and re-layouts  7.55 us (4%)
  other arithmetic  2.06 us (1%)
    pallas_call x1, Pallas kernels, factor_of(): pl.pallas_call(factor_kernel, out_shape=shape((k, k), BF16), grid_spec=pl...  18.7 us
    pallas_call x4, Pallas kernels, op_chunk(): pl.pallas_call(functools.partial(op_kernel, j=j, per=per, count=count), o...  18.7 us
    all_to_all x3, starting transfers between devices, plane(): lax.all_to_all(value, 'rows', 0, 0, tiled=True, axis_index_groups=PLANE)  17.9 us
    ppermute x12, starting transfers between devices, along_cols(): return lax.ppermute(value, 'cols', [(i, (i + s) % Y) for i in range(Y)])  17.4 us
    all_to_all x3, waiting for transfers between devices, plane(): lax.all_to_all(value, 'rows', 0, 0, tiled=True, axis_index_groups=PLANE)  12.6 us
    ppermute x12, waiting for transfers between devices, along_cols(): return lax.ppermute(value, 'cols', [(i, (i + s) % Y) for i in range(Y)])  10.9 us
    all_to_all x1, blocking collectives, plane(): lax.all_to_all(value, 'rows', 0, 0, tiled=True, axis_index_groups=PLANE)  10.1 us
    ppermute x4, starting transfers between devices, flip(): return lax.ppermute(value, 'rows', over_rows(lambda x, z, c: (x, z, c + 1)))  9.72 us
  transfers between devices with their start and end apart: 23, of which 8 were waited for; matrix products, arithmetic and copies ran while one was open for 2% of the time, Pallas kernels for 31%

profile of v2, /device:TPU:1, one launch (start us, length us, event | category | flops | bytes accessed | tf_op | source)
XLA Modules:
  0.0 170.1 jit_solution(14281530723464126950)
XLA Ops:
  0.6 0.9 fusion
  1.5 4.9 %collective-permute-start = (bf16[256,128]{1,0:T(8,128)(2,1)S(1)}, bf16[256,128]{1,0:T(8,128)(2,1)S(1)}, u32[]{:S(2)}, u32[]{:S(2)}) collective-permute-start(bf16[256,128]{1,0:T(8,128)(2,1)S(1)} %get-tuple-element.25), channel_id=1, source_target_pairs={{0,4},{4,8},{8,12},{12,16},{16,20},{20,24},{24,28},{28,32},{32,36}... | collective-permute-start | bytes 196616 | tf_op jit(solution)/shard_map/ppermute | solution.py:515
  6.5 1.9 %collective-permute-start.1 = (bf16[256,128]{1,0:T(8,128)(2,1)S(1)}, bf16[256,128]{1,0:T(8,128)(2,1)S(1)}, u32[]{:S(2)}, u32[]{:S(2)}) collective-permute-start(bf16[256,128]{1,0:T(8,128)(2,1)S(1)} %get-tuple-element.24), channel_id=1, source_target_pairs={{4,0},{8,4},{12,8},{16,12},{20,16},{24,20},{28,24},{32,28},{36,32}... | collective-permute-start | bytes 196616 | tf_op jit(solution)/shard_map/ppermute | solution.py:516
  9.0 3.0 %collective-permute-done.1.high = bf16[256,128]{1,0:T(8,128)(2,1)S(1)} collective-permute-done((bf16[256,128]{1,0:T(8,128)(2,1)S(1)}, bf16[256,128]{1,0:T(8,128)(2,1)S(1)}, u32[]{:S(2)}, u32[]{:S(2)}) %collective-permute-start.1) | collective-permute-done | bytes 65568 | tf_op jit(solution)/shard_map/ppermute | solution.py:516
  12.7 4.7 %op1.1 = bf16[2048,128]{1,0:T(8,128)(2,1)} custom-call(s32[2]{0:T(128)} %pad_add_fusion.meta, bf16[8192,128]{1,0:T(8,128)(2,1)} %nxt.7, bf16[8192,128]{1,0:T(8,128)(2,1)} %nxt.7, bf16[8192,128]{1,0:T(8,128)(2,1)} %nxt.7, bf16[256,128]{1,0:T(8,128)(2,1)} %copy-done.7, bf16[256,128]{1,0:T(8,128)(2,1)} %copy-done.8, bf16[32,256,256]{2,1,0:T(8,128)(2,1)} %lower.9, ...), custom_call_target="tpu_custom_call" | custom-call | flops 536870912 | bytes 5242880 | tf_op jit(solution)/shard_map/op1/pallas_call | solution.py:142
  17.3 1.3 collective-permute-start.2
  18.6 4.7 %op2.1 = bf16[2048,128]{1,0:T(8,128)(2,1)} custom-call(s32[2]{0:T(128)} %pad_add_fusion.meta, bf16[8192,128]{1,0:T(8,128)(2,1)} %nxt.7, bf16[8192,128]{1,0:T(8,128)(2,1)} %nxt.7, bf16[8192,128]{1,0:T(8,128)(2,1)} %nxt.7, bf16[256,128]{1,0:T(8,128)(2,1)} %copy-done.7, bf16[256,128]{1,0:T(8,128)(2,1)} %copy-done.8, bf16[32,256,256]{2,1,0:T(8,128)(2,1)} %lower.9, ...), custom_call_target="tpu_custom_call" | custom-call | flops 536870912 | bytes 5242880 | tf_op jit(solution)/shard_map/op2/pallas_call | solution.py:142
  23.3 2.6 %collective-permute-start.3 = (bf16[2048,128]{1,0:T(8,128)(2,1)}, bf16[2048,128]{1,0:T(8,128)(2,1)S(1)}, u32[]{:S(2)}, u32[]{:S(2)}) collective-permute-start(bf16[2048,128]{1,0:T(8,128)(2,1)} %op2.1), channel_id=1, source_target_pairs={{0,2},{1,3},{2,0},{3,1},{4,6},{5,7},{6,4},{7,5},{8,10},{9,11},{10,... | collective-permute-start | bytes 1572872 | tf_op jit(solution)/shard_map/ppermute | solution.py:60
  25.9 4.7 %op3.1 = bf16[2048,128]{1,0:T(8,128)(2,1)} custom-call(s32[2]{0:T(128)} %pad_add_fusion.meta, bf16[8192,128]{1,0:T(8,128)(2,1)} %nxt.7, bf16[8192,128]{1,0:T(8,128)(2,1)} %nxt.7, bf16[8192,128]{1,0:T(8,128)(2,1)} %nxt.7, bf16[256,128]{1,0:T(8,128)(2,1)} %copy-done.7, bf16[256,128]{1,0:T(8,128)(2,1)} %copy-done.8, bf16[32,256,256]{2,1,0:T(8,128)(2,1)} %lower.9, ...), custom_call_target="tpu_custom_call" | custom-call | flops 536870912 | bytes 5242880 | tf_op jit(solution)/shard_map/op3/pallas_call | solution.py:142
  30.6 1.1 collective-permute-start.4
  31.7 4.7 %op0.1.p0 = bf16[2048,128]{1,0:T(8,128)(2,1)} custom-call(s32[2]{0:T(128)} %pad_add_fusion.meta, bf16[8192,128]{1,0:T(8,128)(2,1)} %nxt.7, bf16[8192,128]{1,0:T(8,128)(2,1)} %nxt.7, bf16[8192,128]{1,0:T(8,128)(2,1)} %nxt.7, bf16[256,128]{1,0:T(8,128)(2,1)} %copy-done.7, bf16[256,128]{1,0:T(8,128)(2,1)} %copy-done.8, bf16[32,256,256]{2,1,0:T(8,128)(2,1)} %lower.9, ...), custom_call_target="tpu_custom_call" | custom-call | flops 536870912 | bytes 5242880 | tf_op jit(solution)/shard_map/op0/pallas_call | solution.py:142
  36.4 6.5 %collective-permute-done.3.p2 = bf16[2048,128]{1,0:T(8,128)(2,1)S(1)} collective-permute-done((bf16[2048,128]{1,0:T(8,128)(2,1)}, bf16[2048,128]{1,0:T(8,128)(2,1)S(1)}, u32[]{:S(2)}, u32[]{:S(2)}) %collective-permute-start.3) | collective-permute-done | bytes 524320 | tf_op jit(solution)/shard_map/ppermute | solution.py:60
  42.9 4.3 %collective-permute-done.4.p3 = bf16[2048,128]{1,0:T(8,128)(2,1)S(1)} collective-permute-done((bf16[2048,128]{1,0:T(8,128)(2,1)}, bf16[2048,128]{1,0:T(8,128)(2,1)S(1)}, u32[]{:S(2)}, u32[]{:S(2)}) %collective-permute-start.4) | collective-permute-done | bytes 524320 | tf_op jit(solution)/shard_map/ppermute | solution.py:60
  47.3 1.0 copy-done.3
  48.3 2.4 %gram.1 = (bf16[2048,512]{1,0:T(8,128)(2,1)S(1)}, bf16[256,512]{1,0:T(8,128)(2,1)S(1)}, bf16[256,512]{1,0:T(8,128)(2,1)S(1)}, f32[640,128]{1,0:T(8,128)S(1)}, f32[640,128]{1,0:T(8,128)S(1)}) custom-call(s32[2]{0:T(128)S(1)} %copy-done.4, bf16[2048,128]{1,0:T(8,128)(2,1)S(1)} %copy-done.3, bf16[2048,128]{1,0:T(8,128)(2,1)S(1)} %collective-permute-done.2.p1, ...), custom_call_target="tpu_custom_call" | custom-call | flops 1073741824 | bytes 5242880 | tf_op jit(solution)/shard_map/gram/pallas_call | solution.py:195
  50.7 1.3 copy-done
  52.0 1.6 collective-permute-done.5
  53.6 0.8 add.21
  54.4 8.5 %all-to-all-start = ((f32[16,40,128]{2,1,0:T(8,128)}), f32[16,40,128]{2,1,0:T(8,128)S(1)}, u32[]{:S(2)}, u32[]{:S(2)}) async-start(f32[16,40,128]{2,1,0:T(8,128)} %bitcast.2), calls=%async_computation | async-start | bytes 655360 | tf_op jit(solution)/shard_map/all_to_all | solution.py:56
  62.9 4.5 %collective-permute-start.13 = (bf16[256,512]{1,0:T(8,128)(2,1)S(1)}, bf16[256,512]{1,0:T(8,128)(2,1)S(1)}, u32[]{:S(2)}, u32[]{:S(2)}) collective-permute-start(bf16[256,512]{1,0:T(8,128)(2,1)S(1)} %get-tuple-element.20), channel_id=1, source_target_pairs={{0,1},{1,2},{2,3},{3,4},{4,5},{5,6},{6,7},{7,8},{8,9},{9,10},{10,1... | collective-permute-start | bytes 786440 | tf_op jit(solution)/shard_map/ppermute | solution.py:65
  67.3 2.6 %collective-permute-start.14 = (bf16[256,512]{1,0:T(8,128)(2,1)S(1)}, bf16[256,512]{1,0:T(8,128)(2,1)S(1)}, u32[]{:S(2)}, u32[]{:S(2)}) collective-permute-start(bf16[256,512]{1,0:T(8,128)(2,1)S(1)} %get-tuple-element.21), channel_id=1, source_target_pairs={{1,0},{2,1},{3,2},{4,3},{5,4},{6,5},{7,6},{8,7},{9,8},{10,9},{11,1... | collective-permute-start | bytes 786440 | tf_op jit(solution)/shard_map/ppermute | solution.py:65
  69.9 1.1 all-to-all-done
  71.1 3.0 %collective-permute-start.6 = (f32[40,128]{1,0:T(8,128)S(1)}, f32[40,128]{1,0:T(8,128)S(1)}, u32[]{:S(2)}, u32[]{:S(2)}) collective-permute-start(f32[40,128]{1,0:T(8,128)S(1)} %reduce_sum.18), channel_id=1, source_target_pairs={{0,2},{1,3},{2,0},{3,1},{4,6},{5,7},{6,4},{7,5},{8,10},{9,11},{10,... | collective-permute-start | bytes 61448 | tf_op jit(solution)/shard_map/ppermute | solution.py:60
  74.1 2.6 %collective-permute-start.8 = (f32[40,128]{1,0:T(8,128)S(1)}, f32[40,128]{1,0:T(8,128)S(1)}, u32[]{:S(2)}, u32[]{:S(2)}) collective-permute-start(f32[40,128]{1,0:T(8,128)S(1)} %reduce_sum.18), channel_id=1, source_target_pairs={{0,3},{1,0},{2,1},{3,2},{4,7},{5,4},{6,5},{7,6},{8,11},{9,8},{10,9... | collective-permute-start | bytes 61448 | tf_op jit(solution)/shard_map/ppermute | solution.py:60
  77.5 8.5 %moment.1 = (f32[256,512]{1,0:T(8,128)}, f32[256,512]{1,0:T(8,128)}) custom-call(s32[2]{0:T(128)} %pad_add_fusion.meta, bf16[2048,512]{1,0:T(8,128)(2,1)} %copy-done, bf16[2048,512]{1,0:T(8,128)(2,1)} %copy-done, bf16[2048,512]{1,0:T(8,128)(2,1)} %copy-done, bf16[256,512]{1,0:T(8,128)(2,1)} %copy-done.11, bf16[256,512]{1,0:T(8,128)(2,1)} %copy-done.12, ...), custom_call_target="tpu_custom_call" | custom-call | flops 3221225472 | bytes 4194304 | tf_op jit(solution)/shard_map/moment/pallas_call | solution.py:250
  86.0 2.8 %collective-permute-start.15 = (f32[256,512]{1,0:T(8,128)}, f32[256,512]{1,0:T(8,128)S(1)}, u32[]{:S(2)}, u32[]{:S(2)}) collective-permute-start(f32[256,512]{1,0:T(8,128)} %get-tuple-element.23), channel_id=1, source_target_pairs={{0,4},{4,0},{8,12},{12,8},{16,20},{20,16},{24,28},{28,24},{32,36},... | collective-permute-start | bytes 1572872 | tf_op jit(solution)/shard_map/ppermute | solution.py:49
  88.9 0.8 broadcast_in_dim.4
  89.6 5.4 %all-to-all-start.1 = ((f32[16,40,128]{2,1,0:T(8,128)}), f32[16,40,128]{2,1,0:T(8,128)S(1)}, u32[]{:S(2)}, u32[]{:S(2)}) async-start(f32[16,40,128]{2,1,0:T(8,128)} %broadcast_in_dim.4), calls=%async_computation.1 | async-start | bytes 655360 | tf_op jit(solution)/shard_map/all_to_all | solution.py:56
  95.1 0.8 copy-done.9
  95.9 2.0 %pack.1 = bf16[16,64,128]{2,1,0:T(8,128)(2,1)} custom-call(f32[256,512]{1,0:T(8,128)} %get-tuple-element.22.keep, f32[256,512]{1,0:T(8,128)} %copy-done.9), custom_call_target="tpu_custom_call" | custom-call | flops 131072 | bytes 1572864 | tf_op jit(solution)/shard_map/pack/pallas_call | solution.py:97
  97.8 5.6 %all-to-all-done.1.mine = f32[16,40,128]{2,1,0:T(8,128)S(1)} async-done(((f32[16,40,128]{2,1,0:T(8,128)}), f32[16,40,128]{2,1,0:T(8,128)S(1)}, u32[]{:S(2)}, u32[]{:S(2)}) %all-to-all-start.1) | async-done | bytes 327712 | tf_op jit(solution)/shard_map/all_to_all | solution.py:56
  103.4 4.0 %all-to-all-start.2 = ((bf16[16,64,128]{2,1,0:T(8,128)(2,1)}), bf16[16,64,128]{2,1,0:T(8,128)(2,1)S(1)}, u32[]{:S(2)}, u32[]{:S(2)}) async-start(bf16[16,64,128]{2,1,0:T(8,128)(2,1)} %pack.1), calls=%async_computation.2 | async-start | bytes 524288 | tf_op jit(solution)/shard_map/all_to_all | solution.py:56
  107.4 1.5 collective-permute-start.9
  108.9 5.9 %all-to-all-done.2 = bf16[16,64,128]{2,1,0:T(8,128)(2,1)S(1)} async-done(((bf16[16,64,128]{2,1,0:T(8,128)(2,1)}), bf16[16,64,128]{2,1,0:T(8,128)(2,1)S(1)}, u32[]{:S(2)}, u32[]{:S(2)}) %all-to-all-start.2) | async-done | bytes 262176 | tf_op jit(solution)/shard_map/all_to_all | solution.py:56
  114.8 1.4 collective-permute-start.16
  116.2 1.2 collective-permute-start.17
  117.4 1.5 collective-permute-start.18
  118.9 18.7 %factor.1.linv = bf16[512,512]{1,0:T(8,128)(2,1)S(1)} custom-call(s32[2]{0:T(128)S(1)} %copy-done.5, f32[16,40,128]{2,1,0:T(8,128)S(1)} %all-to-all-done.1.mine, f32[16,40,128]{2,1,0:T(8,128)S(1)} %collective-permute-done.9.other), custom_call_target="tpu_custom_call" | custom-call | flops 134217728 | bytes 3145728 | tf_op jit(solution)/shard_map/factor/pallas_call | solution.py:384
  137.7 3.5 %ortho.1 = (bf16[2048,128]{1,0:T(8,128)(2,1)S(1)}, bf16[2048,128]{1,0:T(8,128)(2,1)}, bf16[2048,128]{1,0:T(8,128)(2,1)}, bf16[2048,128]{1,0:T(8,128)(2,1)}) custom-call(s32[2]{0:T(128)S(1)} %copy-done.5, bf16[512,512]{1,0:T(8,128)(2,1)S(1)} %factor.1.linv, bf16[2048,512]{1,0:T(8,128)(2,1)S(1)} %copy-done.1), custom_call_target="tpu_custom_call" | custom-call | flops 1073741824 | bytes 4194304 | tf_op jit(solution)/shard_map/ortho/pallas_call | solution.py:415
  141.2 1.2 collective-permute-start.11
  142.4 1.5 collective-permute-start.12
  144.5 2.6 %tail.1 = f32[16,128]{1,0:T(8,128)} custom-call(s32[2]{0:T(128)} %pad_add_fusion.meta, bf16[512,512]{1,0:T(8,128)(2,1)} %copy-done.2, f32[64,128]{1,0:T(8,128)} %add_add_fusion.moment), custom_call_target="tpu_custom_call" | custom-call | flops 6291456 | bytes 524288 | tf_op jit(solution)/shard_map/tail/pallas_call | solution.py:471
  147.2 0.7 broadcast_in_dim.5
  147.9 10.1 %all_to_all.20.mine = f32[16,16,128]{2,1,0:T(8,128)S(1)} all-to-all(f32[16,16,128]{2,1,0:T(8,128)S(1)} %broadcast_in_dim.5), channel_id=1, replica_groups={{0,8,16,24,32,40,48,56,64,72,80,88,96,104,112,120},{4,12,20,28,36,44,52..., dimensions={0} | all-to-all | bytes 262144 | tf_op jit(solution)/shard_map/all_to_all | solution.py:56
  158.0 5.4 %collective-permute-start.19 = (f32[16,16,128]{2,1,0:T(8,128)S(1)}, f32[16,16,128]{2,1,0:T(8,128)S(1)}, u32[]{:S(2)}, u32[]{:S(2)}) collective-permute-start(f32[16,16,128]{2,1,0:T(8,128)S(1)} %all_to_all.20.mine), channel_id=1, source_target_pairs={{0,4},{4,0},{8,12},{12,8},{16,20},{20,16},{24,28},{28,24},{32,36},... | collective-permute-start | bytes 393224 | tf_op jit(solution)/shard_map/ppermute | solution.py:49
  163.4 1.0 collective-permute-done.19.other
  165.0 3.1 %project.1 = f32[512,128]{1,0:T(8,128)} custom-call(s32[2]{0:T(128)} %pad_add_fusion.meta, bf16[512,512]{1,0:T(8,128)(2,1)} %copy-done.2, f32[16,16,128]{2,1,0:T(8,128)} %copy-done.10, f32[16,16,128]{2,1,0:T(8,128)} %copy-done.13), custom_call_target="tpu_custom_call" | custom-call | flops 201326592 | bytes 1048576 | tf_op jit(solution)/shard_map/project/pallas_call | solution.py:493
  168.1 2.0 %join.1 = bf16[8192,128]{1,0:T(8,128)(2,1)} custom-call(s32[2]{0:T(128)S(1)} %copy-done.6, bf16[2048,128]{1,0:T(8,128)(2,1)S(1)} %get-tuple-element.16.refs_0_, bf16[2048,128]{1,0:T(8,128)(2,1)S(1)} %collective-permute-done.10.refs_1_, bf16[2048,128]{1,0:T(8,128)(2,1)S(1)} %collective-permute-done.11.refs_2_, ...), custom_call_target="tpu_custom_call" | custom-call | bytes 4194304 | tf_op jit(solution)/shard_map/join/pallas_call | solution.py:440
  (48 shorter events, 3.5 us)
Async XLA Ops:
  1.5 7.5 %collective-permute-start = (bf16[256,128]{1,0:T(8,128)(2,1)S(1)}, bf16[256,128]{1,0:T(8,128)(2,1)S(1)}, u32[]{:S(2)}, u32[]{:S(2)}) collective-permute-start(bf16[256,128]{1,0:T(8,128)(2,1)S(1)} %get-tuple-element.25), channel_id=1, source_target_pairs={{0,4},{4,8},{8,12},{12,16},{16,20},{20,24},{24,28},{28,32},{32,36}... | collective-permute-start | bytes 196616 | tf_op jit(solution)/shard_map/ppermute | solution.py:515
  6.5 5.6 %collective-permute-start.1 = (bf16[256,128]{1,0:T(8,128)(2,1)S(1)}, bf16[256,128]{1,0:T(8,128)(2,1)S(1)}, u32[]{:S(2)}, u32[]{:S(2)}) collective-permute-start(bf16[256,128]{1,0:T(8,128)(2,1)S(1)} %get-tuple-element.24), channel_id=1, source_target_pairs={{4,0},{8,4},{12,8},{16,12},{20,16},{24,20},{28,24},{32,28},{36,32}... | collective-permute-start | bytes 196616 | tf_op jit(solution)/shard_map/ppermute | solution.py:516
  9.0 3.1 %copy-start.7 = (bf16[256,128]{1,0:T(8,128)(2,1)}, bf16[256,128]{1,0:T(8,128)(2,1)S(1)}, u32[]{:S(2)}) copy-start(bf16[256,128]{1,0:T(8,128)(2,1)S(1)} %collective-permute-done.low) | copy-start | bytes 196612
  12.0 0.6 copy-start.8
  17.3 19.1 %collective-permute-start.2 = (bf16[2048,128]{1,0:T(8,128)(2,1)}, bf16[2048,128]{1,0:T(8,128)(2,1)S(1)}, u32[]{:S(2)}, u32[]{:S(2)}) collective-permute-start(bf16[2048,128]{1,0:T(8,128)(2,1)} %op1.1), channel_id=1, source_target_pairs={{0,1},{1,2},{2,3},{3,0},{4,5},{5,6},{6,7},{7,4},{8,9},{9,10},{10,1... | collective-permute-start | bytes 1572872 | tf_op jit(solution)/shard_map/ppermute | solution.py:60
  23.3 19.6 %collective-permute-start.3 = (bf16[2048,128]{1,0:T(8,128)(2,1)}, bf16[2048,128]{1,0:T(8,128)(2,1)S(1)}, u32[]{:S(2)}, u32[]{:S(2)}) collective-permute-start(bf16[2048,128]{1,0:T(8,128)(2,1)} %op2.1), channel_id=1, source_target_pairs={{0,2},{1,3},{2,0},{3,1},{4,6},{5,7},{6,4},{7,5},{8,10},{9,11},{10,... | collective-permute-start | bytes 1572872 | tf_op jit(solution)/shard_map/ppermute | solution.py:60
  30.6 16.7 %copy-start.4 = (s32[2]{0:T(128)S(1)}, s32[2]{0:T(128)}, u32[]{:S(2)}) copy-start(s32[2]{0:T(128)} %pad_add_fusion.meta) | copy-start | bytes 28
  30.6 16.7 %collective-permute-start.4 = (bf16[2048,128]{1,0:T(8,128)(2,1)}, bf16[2048,128]{1,0:T(8,128)(2,1)S(1)}, u32[]{:S(2)}, u32[]{:S(2)}) collective-permute-start(bf16[2048,128]{1,0:T(8,128)(2,1)} %op3.1), channel_id=1, source_target_pairs={{0,3},{1,0},{2,1},{3,2},{4,7},{5,4},{6,5},{7,6},{8,11},{9,8},{10,9... | collective-permute-start | bytes 1572872 | tf_op jit(solution)/shard_map/ppermute | solution.py:60
  47.3 1.0 copy-start.3
  50.7 1.3 copy-start
  52.0 1.6 collective-permute-start.5
  54.4 16.7 %all-to-all-start = ((f32[16,40,128]{2,1,0:T(8,128)}), f32[16,40,128]{2,1,0:T(8,128)S(1)}, u32[]{:S(2)}, u32[]{:S(2)}) async-start(f32[16,40,128]{2,1,0:T(8,128)} %bitcast.2), calls=%async_computation | async-start | bytes 655360 | tf_op jit(solution)/shard_map/all_to_all | solution.py:56
  62.9 13.9 %collective-permute-start.13 = (bf16[256,512]{1,0:T(8,128)(2,1)S(1)}, bf16[256,512]{1,0:T(8,128)(2,1)S(1)}, u32[]{:S(2)}, u32[]{:S(2)}) collective-permute-start(bf16[256,512]{1,0:T(8,128)(2,1)S(1)} %get-tuple-element.20), channel_id=1, source_target_pairs={{0,1},{1,2},{2,3},{3,4},{4,5},{5,6},{6,7},{7,8},{8,9},{9,10},{10,1... | collective-permute-start | bytes 786440 | tf_op jit(solution)/shard_map/ppermute | solution.py:65
  67.3 9.4 %collective-permute-start.14 = (bf16[256,512]{1,0:T(8,128)(2,1)S(1)}, bf16[256,512]{1,0:T(8,128)(2,1)S(1)}, u32[]{:S(2)}, u32[]{:S(2)}) collective-permute-start(bf16[256,512]{1,0:T(8,128)(2,1)S(1)} %get-tuple-element.21), channel_id=1, source_target_pairs={{1,0},{2,1},{3,2},{4,3},{5,4},{6,5},{7,6},{8,7},{9,8},{10,9},{11,1... | collective-permute-start | bytes 786440 | tf_op jit(solution)/shard_map/ppermute | solution.py:65
  71.1 17.8 %collective-permute-start.6 = (f32[40,128]{1,0:T(8,128)S(1)}, f32[40,128]{1,0:T(8,128)S(1)}, u32[]{:S(2)}, u32[]{:S(2)}) collective-permute-start(f32[40,128]{1,0:T(8,128)S(1)} %reduce_sum.18), channel_id=1, source_target_pairs={{0,2},{1,3},{2,0},{3,1},{4,6},{5,7},{6,4},{7,5},{8,10},{9,11},{10,... | collective-permute-start | bytes 61448 | tf_op jit(solution)/shard_map/ppermute | solution.py:60
  74.1 14.8 %collective-permute-start.7 = (f32[40,128]{1,0:T(8,128)S(1)}, f32[40,128]{1,0:T(8,128)S(1)}, u32[]{:S(2)}, u32[]{:S(2)}) collective-permute-start(f32[40,128]{1,0:T(8,128)S(1)} %reduce_sum.18), channel_id=1, source_target_pairs={{0,1},{1,2},{2,3},{3,0},{4,5},{5,6},{6,7},{7,4},{8,9},{9,10},{10,1... | collective-permute-start | bytes 61448 | tf_op jit(solution)/shard_map/ppermute | solution.py:60
  74.1 14.7 %collective-permute-start.8 = (f32[40,128]{1,0:T(8,128)S(1)}, f32[40,128]{1,0:T(8,128)S(1)}, u32[]{:S(2)}, u32[]{:S(2)}) collective-permute-start(f32[40,128]{1,0:T(8,128)S(1)} %reduce_sum.18), channel_id=1, source_target_pairs={{0,3},{1,0},{2,1},{3,2},{4,7},{5,4},{6,5},{7,6},{8,11},{9,8},{10,9... | collective-permute-start | bytes 61448 | tf_op jit(solution)/shard_map/ppermute | solution.py:60
  76.7 0.7 copy-start.11
  76.7 0.8 copy-start.12
  77.5 41.4 %copy-start.5 = (s32[2]{0:T(128)S(1)}, s32[2]{0:T(128)}, u32[]{:S(2)}) copy-start(s32[2]{0:T(128)} %pad_add_fusion.meta) | copy-start | bytes 28
  86.0 51.7 %copy-start.1 = (bf16[2048,512]{1,0:T(8,128)(2,1)S(1)}, bf16[2048,512]{1,0:T(8,128)(2,1)}, u32[]{:S(2)}) copy-start(bf16[2048,512]{1,0:T(8,128)(2,1)} %copy-done) | copy-start | bytes 6291460
  86.0 9.1 %collective-permute-start.15 = (f32[256,512]{1,0:T(8,128)}, f32[256,512]{1,0:T(8,128)S(1)}, u32[]{:S(2)}, u32[]{:S(2)}) collective-permute-start(f32[256,512]{1,0:T(8,128)} %get-tuple-element.23), channel_id=1, source_target_pairs={{0,4},{4,0},{8,12},{12,8},{16,20},{20,16},{24,28},{28,24},{32,36},... | collective-permute-start | bytes 1572872 | tf_op jit(solution)/shard_map/ppermute | solution.py:49
  89.6 13.8 %all-to-all-start.1 = ((f32[16,40,128]{2,1,0:T(8,128)}), f32[16,40,128]{2,1,0:T(8,128)S(1)}, u32[]{:S(2)}, u32[]{:S(2)}) async-start(f32[16,40,128]{2,1,0:T(8,128)} %broadcast_in_dim.4), calls=%async_computation.1 | async-start | bytes 655360 | tf_op jit(solution)/shard_map/all_to_all | solution.py:56
  95.1 0.8 copy-start.9
  97.8 70.3 %copy-start.6 = (s32[2]{0:T(128)S(1)}, s32[2]{0:T(128)}, u32[]{:S(2)}) copy-start(s32[2]{0:T(128)} %pad_add_fusion.meta) | copy-start | bytes 28
  103.4 11.4 %all-to-all-start.2 = ((bf16[16,64,128]{2,1,0:T(8,128)(2,1)}), bf16[16,64,128]{2,1,0:T(8,128)(2,1)S(1)}, u32[]{:S(2)}, u32[]{:S(2)}) async-start(bf16[16,64,128]{2,1,0:T(8,128)(2,1)} %pack.1), calls=%async_computation.2 | async-start | bytes 524288 | tf_op jit(solution)/shard_map/all_to_all | solution.py:56
  107.4 11.5 %collective-permute-start.9 = (f32[16,40,128]{2,1,0:T(8,128)S(1)}, f32[16,40,128]{2,1,0:T(8,128)S(1)}, u32[]{:S(2)}, u32[]{:S(2)}) collective-permute-start(f32[16,40,128]{2,1,0:T(8,128)S(1)} %all-to-all-done.1.mine), channel_id=1, source_target_pairs={{0,4},{4,0},{8,12},{12,8},{16,20},{20,16},{24,28},{28,24},{32,36},... | collective-permute-start | bytes 983048 | tf_op jit(solution)/shard_map/ppermute | solution.py:49
  114.8 27.6 %collective-permute-start.16 = (f32[64,128]{1,0:T(8,128)S(1)}, f32[64,128]{1,0:T(8,128)S(1)}, u32[]{:S(2)}, u32[]{:S(2)}) collective-permute-start(f32[64,128]{1,0:T(8,128)S(1)} %convert_reduce_fusion), channel_id=1, source_target_pairs={{0,2},{1,3},{2,0},{3,1},{4,6},{5,7},{6,4},{7,5},{8,10},{9,11},{10,... | collective-permute-start | bytes 98312 | tf_op jit(solution)/shard_map/ppermute | solution.py:60
  116.2 27.7 %collective-permute-start.17 = (f32[64,128]{1,0:T(8,128)S(1)}, f32[64,128]{1,0:T(8,128)S(1)}, u32[]{:S(2)}, u32[]{:S(2)}) collective-permute-start(f32[64,128]{1,0:T(8,128)S(1)} %convert_reduce_fusion), channel_id=1, source_target_pairs={{0,1},{1,2},{2,3},{3,0},{4,5},{5,6},{6,7},{7,4},{8,9},{9,10},{10,1... | collective-permute-start | bytes 98312 | tf_op jit(solution)/shard_map/ppermute | solution.py:60
  117.4 26.5 %collective-permute-start.18 = (f32[64,128]{1,0:T(8,128)S(1)}, f32[64,128]{1,0:T(8,128)S(1)}, u32[]{:S(2)}, u32[]{:S(2)}) collective-permute-start(f32[64,128]{1,0:T(8,128)S(1)} %convert_reduce_fusion), channel_id=1, source_target_pairs={{0,3},{1,0},{2,1},{3,2},{4,7},{5,4},{6,5},{7,6},{8,11},{9,8},{10,9... | collective-permute-start | bytes 98312 | tf_op jit(solution)/shard_map/ppermute | solution.py:60
  137.7 6.9 %copy-start.2 = (bf16[512,512]{1,0:T(8,128)(2,1)}, bf16[512,512]{1,0:T(8,128)(2,1)S(1)}, u32[]{:S(2)}) copy-start(bf16[512,512]{1,0:T(8,128)(2,1)S(1)} %factor.1.linv) | copy-start | bytes 1572868
  141.2 26.9 %collective-permute-start.10 = (bf16[2048,128]{1,0:T(8,128)(2,1)}, bf16[2048,128]{1,0:T(8,128)(2,1)S(1)}, u32[]{:S(2)}, u32[]{:S(2)}) collective-permute-start(bf16[2048,128]{1,0:T(8,128)(2,1)} %get-tuple-element.17), channel_id=1, source_target_pairs={{0,1},{1,2},{2,3},{3,0},{4,5},{5,6},{6,7},{7,4},{8,9},{9,10},{10,1... | collective-permute-start | bytes 1572872 | tf_op jit(solution)/shard_map/ppermute | solution.py:60
  141.2 26.9 %collective-permute-start.11 = (bf16[2048,128]{1,0:T(8,128)(2,1)}, bf16[2048,128]{1,0:T(8,128)(2,1)S(1)}, u32[]{:S(2)}, u32[]{:S(2)}) collective-permute-start(bf16[2048,128]{1,0:T(8,128)(2,1)} %get-tuple-element.18), channel_id=1, source_target_pairs={{0,2},{1,3},{2,0},{3,1},{4,6},{5,7},{6,4},{7,5},{8,10},{9,11},{10,... | collective-permute-start | bytes 1572872 | tf_op jit(solution)/shard_map/ppermute | solution.py:60
  142.4 25.7 %collective-permute-start.12 = (bf16[2048,128]{1,0:T(8,128)(2,1)}, bf16[2048,128]{1,0:T(8,128)(2,1)S(1)}, u32[]{:S(2)}, u32[]{:S(2)}) collective-permute-start(bf16[2048,128]{1,0:T(8,128)(2,1)} %get-tuple-element.19), channel_id=1, source_target_pairs={{0,3},{1,0},{2,1},{3,2},{4,7},{5,4},{6,5},{7,6},{8,11},{9,8},{10,9... | collective-permute-start | bytes 1572872 | tf_op jit(solution)/shard_map/ppermute | solution.py:60
  158.0 6.4 %copy-start.10 = (f32[16,16,128]{2,1,0:T(8,128)}, f32[16,16,128]{2,1,0:T(8,128)S(1)}, u32[]{:S(2)}) copy-start(f32[16,16,128]{2,1,0:T(8,128)S(1)} %all_to_all.20.mine) | copy-start | bytes 393220
  158.0 6.4 %collective-permute-start.19 = (f32[16,16,128]{2,1,0:T(8,128)S(1)}, f32[16,16,128]{2,1,0:T(8,128)S(1)}, u32[]{:S(2)}, u32[]{:S(2)}) collective-permute-start(f32[16,16,128]{2,1,0:T(8,128)S(1)} %all_to_all.20.mine), channel_id=1, source_target_pairs={{0,4},{4,0},{8,12},{12,8},{16,20},{20,16},{24,28},{28,24},{32,36},... | collective-permute-start | bytes 393224 | tf_op jit(solution)/shard_map/ppermute | solution.py:49
  164.4 0.6 copy-start.13

commit v3 on v2

--- a/solution.py
+++ b/solution.py
@@ -236,7 +236,7 @@
         half = acc.shape[0] // 2
         core = meta[1]
         keep[...] = acc[pl.ds(pl.multiple_of(core * half, 8), half), :]
-        send[...] = acc[pl.ds(pl.multiple_of((1 - core) * half, 8), half), :]
+        send[...] = acc[pl.ds(pl.multiple_of((1 - core) * half, 8), half), :].astype(BF16)
 
 
 def moment_of(meta, wide, low, high, lower, diag, upper, inverse):
@@ -249,7 +249,7 @@
     out = pl.BlockSpec((k // 2, k), lambda i, m: (0, 0))
     return pl.pallas_call(
         moment_kernel,
-        out_shape=(shape((k // 2, k), F32), shape((k // 2, k), F32)),
+        out_shape=(shape((k // 2, k), F32), shape((k // 2, k), BF16)),
         grid_spec=pltpu.PrefetchScalarGridSpec(
             num_scalar_prefetch=1,
             grid=(steps,),

time: 171 us -> 171 us (level)
  starting transfers between devices: 59 us -> 61.5 us
  waiting for transfers between devices: 29.1 us -> 26.7 us
    all_to_all x3, waiting for transfers between devices: 12.6 us -> 7.82 us  [plane(): lax.all_to_all(value, 'rows', 0, 0, tiled=True, axis_index_groups=PLANE)]
    all_to_all x3, starting transfers between devices: 17.9 us -> 21.9 us  [plane(): lax.all_to_all(value, 'rows', 0, 0, tiled=True, axis_index_groups=PLANE)]
    ppermute x12, waiting for transfers between devices: 10.9 us -> 14.4 us  [along_cols(): return lax.ppermute(value, 'cols', [(i, (i + s) % Y) for i in range(Y)])]
    ppermute x1, waiting for transfers between devices: 3.05 us -> 0.01 us  [shards(): high = lax.ppermute(basis[:size], 'rows', [(b, a) for a, b in forward])]
  transfers between devices with their start and end apart: 23 -> 23, of which waited for: 8 -> 11; matrix products, arithmetic and copies ran while one was open for 2% -> 2% of each run, Pallas kernels for 31% -> 31%
where the time goes in v3:
time: 171 us; the launch traced here: 170 us
  starting transfers between devices  61.5 us (36%)
  Pallas kernels  61.3 us (36%)
  waiting for transfers between devices  26.7 us (16%)
  blocking collectives  10.2 us (6%)
  local copies, waits for them, and re-layouts  7.48 us (4%)
  other arithmetic  2.06 us (1%)
    all_to_all x3, starting transfers between devices, plane(): lax.all_to_all(value, 'rows', 0, 0, tiled=True, axis_index_groups=PLANE)  21.9 us
    pallas_call x1, Pallas kernels, factor_of(): pl.pallas_call(factor_kernel, out_shape=shape((k, k), BF16), grid_spec=pl...  18.7 us
    pallas_call x4, Pallas kernels, op_chunk(): pl.pallas_call(functools.partial(op_kernel, j=j, per=per, count=count), o...  18.7 us
    ppermute x12, starting transfers between devices, along_cols(): return lax.ppermute(value, 'cols', [(i, (i + s) % Y) for i in range(Y)])  17.5 us
    ppermute x12, waiting for transfers between devices, along_cols(): return lax.ppermute(value, 'cols', [(i, (i + s) % Y) for i in range(Y)])  14.4 us
    all_to_all x1, blocking collectives, plane(): lax.all_to_all(value, 'rows', 0, 0, tiled=True, axis_index_groups=PLANE)  10.2 us
    pallas_call x1, Pallas kernels, moment_of(): pl.pallas_call(moment_kernel, out_shape=(shape((k // 2, k), F32), shape((...  8.37 us
    ppermute x4, starting transfers between devices, flip(): return lax.ppermute(value, 'rows', over_rows(lambda x, z, c: (x, z, c + 1)))  8.35 us
  transfers between devices with their start and end apart: 23, of which 11 were waited for; matrix products, arithmetic and copies ran while one was open for 2% of the time, Pallas kernels for 31%

profile of v3, /device:TPU:1, one launch (start us, length us, event | category | flops | bytes accessed | tf_op | source)
XLA Modules:
  0.0 170.0 jit_solution(1495036743081306749)
XLA Ops:
  0.6 0.9 fusion
  1.5 3.3 %collective-permute-start.1 = (bf16[256,128]{1,0:T(8,128)(2,1)S(1)}, bf16[256,128]{1,0:T(8,128)(2,1)S(1)}, u32[]{:S(2)}, u32[]{:S(2)}) collective-permute-start(bf16[256,128]{1,0:T(8,128)(2,1)S(1)} %get-tuple-element.24), channel_id=1, source_target_pairs={{4,0},{8,4},{12,8},{16,12},{20,16},{24,20},{28,24},{32,28},{36,32}... | collective-permute-start | bytes 196616 | tf_op jit(solution)/shard_map/ppermute | solution.py:516
  4.9 3.5 %collective-permute-start = (bf16[256,128]{1,0:T(8,128)(2,1)S(1)}, bf16[256,128]{1,0:T(8,128)(2,1)S(1)}, u32[]{:S(2)}, u32[]{:S(2)}) collective-permute-start(bf16[256,128]{1,0:T(8,128)(2,1)S(1)} %get-tuple-element.25), channel_id=1, source_target_pairs={{0,4},{4,8},{8,12},{12,16},{16,20},{20,24},{24,28},{28,32},{32,36}... | collective-permute-start | bytes 196616 | tf_op jit(solution)/shard_map/ppermute | solution.py:515
  9.0 0.7 collective-permute-done.low
  10.3 4.7 %op1.1 = bf16[2048,128]{1,0:T(8,128)(2,1)} custom-call(s32[2]{0:T(128)} %pad_add_fusion.meta, bf16[8192,128]{1,0:T(8,128)(2,1)} %nxt.7, bf16[8192,128]{1,0:T(8,128)(2,1)} %nxt.7, bf16[8192,128]{1,0:T(8,128)(2,1)} %nxt.7, bf16[256,128]{1,0:T(8,128)(2,1)} %copy-done.8, bf16[256,128]{1,0:T(8,128)(2,1)} %copy-done.7, bf16[32,256,256]{2,1,0:T(8,128)(2,1)} %lower.9, ...), custom_call_target="tpu_custom_call" | custom-call | flops 536870912 | bytes 5242880 | tf_op jit(solution)/shard_map/op1/pallas_call | solution.py:142
  15.0 1.3 collective-permute-start.2
  16.3 4.7 %op2.1 = bf16[2048,128]{1,0:T(8,128)(2,1)} custom-call(s32[2]{0:T(128)} %pad_add_fusion.meta, bf16[8192,128]{1,0:T(8,128)(2,1)} %nxt.7, bf16[8192,128]{1,0:T(8,128)(2,1)} %nxt.7, bf16[8192,128]{1,0:T(8,128)(2,1)} %nxt.7, bf16[256,128]{1,0:T(8,128)(2,1)} %copy-done.8, bf16[256,128]{1,0:T(8,128)(2,1)} %copy-done.7, bf16[32,256,256]{2,1,0:T(8,128)(2,1)} %lower.9, ...), custom_call_target="tpu_custom_call" | custom-call | flops 536870912 | bytes 5242880 | tf_op jit(solution)/shard_map/op2/pallas_call | solution.py:142
  21.0 2.6 %collective-permute-start.3 = (bf16[2048,128]{1,0:T(8,128)(2,1)}, bf16[2048,128]{1,0:T(8,128)(2,1)S(1)}, u32[]{:S(2)}, u32[]{:S(2)}) collective-permute-start(bf16[2048,128]{1,0:T(8,128)(2,1)} %op2.1), channel_id=1, source_target_pairs={{0,2},{1,3},{2,0},{3,1},{4,6},{5,7},{6,4},{7,5},{8,10},{9,11},{10,... | collective-permute-start | bytes 1572872 | tf_op jit(solution)/shard_map/ppermute | solution.py:60
  23.6 4.7 %op3.1 = bf16[2048,128]{1,0:T(8,128)(2,1)} custom-call(s32[2]{0:T(128)} %pad_add_fusion.meta, bf16[8192,128]{1,0:T(8,128)(2,1)} %nxt.7, bf16[8192,128]{1,0:T(8,128)(2,1)} %nxt.7, bf16[8192,128]{1,0:T(8,128)(2,1)} %nxt.7, bf16[256,128]{1,0:T(8,128)(2,1)} %copy-done.8, bf16[256,128]{1,0:T(8,128)(2,1)} %copy-done.7, bf16[32,256,256]{2,1,0:T(8,128)(2,1)} %lower.9, ...), custom_call_target="tpu_custom_call" | custom-call | flops 536870912 | bytes 5242880 | tf_op jit(solution)/shard_map/op3/pallas_call | solution.py:142
  28.2 1.1 collective-permute-start.4
  29.4 4.7 %op0.1.p0 = bf16[2048,128]{1,0:T(8,128)(2,1)} custom-call(s32[2]{0:T(128)} %pad_add_fusion.meta, bf16[8192,128]{1,0:T(8,128)(2,1)} %nxt.7, bf16[8192,128]{1,0:T(8,128)(2,1)} %nxt.7, bf16[8192,128]{1,0:T(8,128)(2,1)} %nxt.7, bf16[256,128]{1,0:T(8,128)(2,1)} %copy-done.8, bf16[256,128]{1,0:T(8,128)(2,1)} %copy-done.7, bf16[32,256,256]{2,1,0:T(8,128)(2,1)} %lower.9, ...), custom_call_target="tpu_custom_call" | custom-call | flops 536870912 | bytes 5242880 | tf_op jit(solution)/shard_map/op0/pallas_call | solution.py:142
  34.1 7.8 %collective-permute-done.3.p2 = bf16[2048,128]{1,0:T(8,128)(2,1)S(1)} collective-permute-done((bf16[2048,128]{1,0:T(8,128)(2,1)}, bf16[2048,128]{1,0:T(8,128)(2,1)S(1)}, u32[]{:S(2)}, u32[]{:S(2)}) %collective-permute-start.3) | collective-permute-done | bytes 524320 | tf_op jit(solution)/shard_map/ppermute | solution.py:60
  41.9 4.2 %collective-permute-done.4.p3 = bf16[2048,128]{1,0:T(8,128)(2,1)S(1)} collective-permute-done((bf16[2048,128]{1,0:T(8,128)(2,1)}, bf16[2048,128]{1,0:T(8,128)(2,1)S(1)}, u32[]{:S(2)}, u32[]{:S(2)}) %collective-permute-start.4) | collective-permute-done | bytes 524320 | tf_op jit(solution)/shard_map/ppermute | solution.py:60
  46.1 1.0 copy-done.3
  47.2 2.4 %gram.1 = (bf16[2048,512]{1,0:T(8,128)(2,1)S(1)}, bf16[256,512]{1,0:T(8,128)(2,1)S(1)}, bf16[256,512]{1,0:T(8,128)(2,1)S(1)}, f32[640,128]{1,0:T(8,128)S(1)}, f32[640,128]{1,0:T(8,128)S(1)}) custom-call(s32[2]{0:T(128)S(1)} %copy-done.4, bf16[2048,128]{1,0:T(8,128)(2,1)S(1)} %copy-done.3, bf16[2048,128]{1,0:T(8,128)(2,1)S(1)} %collective-permute-done.2.p1, ...), custom_call_target="tpu_custom_call" | custom-call | flops 1073741824 | bytes 5242880 | tf_op jit(solution)/shard_map/gram/pallas_call | solution.py:195
  49.6 1.3 copy-done
  51.1 1.4 collective-permute-done.5
  52.5 0.8 add.21
  53.3 9.8 %all-to-all-start = ((f32[16,40,128]{2,1,0:T(8,128)}), f32[16,40,128]{2,1,0:T(8,128)S(1)}, u32[]{:S(2)}, u32[]{:S(2)}) async-start(f32[16,40,128]{2,1,0:T(8,128)} %bitcast.2), calls=%async_computation | async-start | bytes 655360 | tf_op jit(solution)/shard_map/all_to_all | solution.py:56
  63.1 4.3 %collective-permute-start.13 = (bf16[256,512]{1,0:T(8,128)(2,1)S(1)}, bf16[256,512]{1,0:T(8,128)(2,1)S(1)}, u32[]{:S(2)}, u32[]{:S(2)}) collective-permute-start(bf16[256,512]{1,0:T(8,128)(2,1)S(1)} %get-tuple-element.20), channel_id=1, source_target_pairs={{0,1},{1,2},{2,3},{3,4},{4,5},{5,6},{6,7},{7,8},{8,9},{9,10},{10,1... | collective-permute-start | bytes 786440 | tf_op jit(solution)/shard_map/ppermute | solution.py:65
  67.4 2.6 %collective-permute-start.14 = (bf16[256,512]{1,0:T(8,128)(2,1)S(1)}, bf16[256,512]{1,0:T(8,128)(2,1)S(1)}, u32[]{:S(2)}, u32[]{:S(2)}) collective-permute-start(bf16[256,512]{1,0:T(8,128)(2,1)S(1)} %get-tuple-element.21), channel_id=1, source_target_pairs={{1,0},{2,1},{3,2},{4,3},{5,4},{6,5},{7,6},{8,7},{9,8},{10,9},{11,1... | collective-permute-start | bytes 786440 | tf_op jit(solution)/shard_map/ppermute | solution.py:65
  70.0 1.0 all-to-all-done
  71.1 2.6 %collective-permute-start.8 = (f32[40,128]{1,0:T(8,128)S(1)}, f32[40,128]{1,0:T(8,128)S(1)}, u32[]{:S(2)}, u32[]{:S(2)}) collective-permute-start(f32[40,128]{1,0:T(8,128)S(1)} %reduce_sum.18), channel_id=1, source_target_pairs={{0,3},{1,0},{2,1},{3,2},{4,7},{5,4},{6,5},{7,6},{8,11},{9,8},{10,9... | collective-permute-start | bytes 61448 | tf_op jit(solution)/shard_map/ppermute | solution.py:60
  73.7 1.9 %collective-permute-start.6 = (f32[40,128]{1,0:T(8,128)S(1)}, f32[40,128]{1,0:T(8,128)S(1)}, u32[]{:S(2)}, u32[]{:S(2)}) collective-permute-start(f32[40,128]{1,0:T(8,128)S(1)} %reduce_sum.18), channel_id=1, source_target_pairs={{0,2},{1,3},{2,0},{3,1},{4,6},{5,7},{6,4},{7,5},{8,10},{9,11},{10,... | collective-permute-start | bytes 61448 | tf_op jit(solution)/shard_map/ppermute | solution.py:60
  75.5 1.1 collective-permute-done.8
  76.6 0.9 collective-permute-done.7
  77.8 0.8 broadcast_in_dim.4
  78.6 5.2 %all-to-all-start.1 = ((f32[16,40,128]{2,1,0:T(8,128)}), f32[16,40,128]{2,1,0:T(8,128)S(1)}, u32[]{:S(2)}, u32[]{:S(2)}) async-start(f32[16,40,128]{2,1,0:T(8,128)} %broadcast_in_dim.4), calls=%async_computation.1 | async-start | bytes 655360 | tf_op jit(solution)/shard_map/all_to_all | solution.py:56
  84.6 8.4 %moment.1 = (f32[256,512]{1,0:T(8,128)}, bf16[256,512]{1,0:T(8,128)(2,1)}) custom-call(s32[2]{0:T(128)} %pad_add_fusion.meta, bf16[2048,512]{1,0:T(8,128)(2,1)} %copy-done, bf16[2048,512]{1,0:T(8,128)(2,1)} %copy-done, bf16[2048,512]{1,0:T(8,128)(2,1)} %copy-done, bf16[256,512]{1,0:T(8,128)(2,1)} %copy-done.10, bf16[256,512]{1,0:T(8,128)(2,1)} %copy-done.11, ...), custom_call_target="tpu_custom_call" | custom-call | flops 3221225472 | bytes 4194304 | tf_op jit(solution)/shard_map/moment/pallas_call | solution.py:250
  93.0 3.1 %collective-permute-start.15 = (bf16[256,512]{1,0:T(8,128)(2,1)}, bf16[256,512]{1,0:T(8,128)(2,1)S(1)}, u32[]{:S(2)}, u32[]{:S(2)}) collective-permute-start(bf16[256,512]{1,0:T(8,128)(2,1)} %get-tuple-element.23), channel_id=1, source_target_pairs={{0,4},{4,0},{8,12},{12,8},{16,20},{20,16},{24,28},{28,24},{32,36},... | collective-permute-start | bytes 786440 | tf_op jit(solution)/shard_map/ppermute | solution.py:49
  96.0 1.4 collective-permute-done.15.got
  98.1 1.9 %pack.1 = bf16[16,64,128]{2,1,0:T(8,128)(2,1)} custom-call(f32[256,512]{1,0:T(8,128)} %get-tuple-element.22.keep, bf16[256,512]{1,0:T(8,128)(2,1)} %copy-done.12), custom_call_target="tpu_custom_call" | custom-call | flops 131072 | bytes 1572864 | tf_op jit(solution)/shard_map/pack/pallas_call | solution.py:97
  100.0 6.9 %all-to-all-start.2 = ((bf16[16,64,128]{2,1,0:T(8,128)(2,1)}), bf16[16,64,128]{2,1,0:T(8,128)(2,1)S(1)}, u32[]{:S(2)}, u32[]{:S(2)}) async-start(bf16[16,64,128]{2,1,0:T(8,128)(2,1)} %pack.1), calls=%async_computation.2 | async-start | bytes 524288 | tf_op jit(solution)/shard_map/all_to_all | solution.py:56
  106.9 0.7 collective-permute-start.9
  107.6 6.8 %all-to-all-done.2 = bf16[16,64,128]{2,1,0:T(8,128)(2,1)S(1)} async-done(((bf16[16,64,128]{2,1,0:T(8,128)(2,1)}), bf16[16,64,128]{2,1,0:T(8,128)(2,1)S(1)}, u32[]{:S(2)}, u32[]{:S(2)}) %all-to-all-start.2) | async-done | bytes 262176 | tf_op jit(solution)/shard_map/all_to_all | solution.py:56
  114.5 2.2 %collective-permute-start.18 = (f32[64,128]{1,0:T(8,128)S(1)}, f32[64,128]{1,0:T(8,128)S(1)}, u32[]{:S(2)}, u32[]{:S(2)}) collective-permute-start(f32[64,128]{1,0:T(8,128)S(1)} %convert_reduce_fusion), channel_id=1, source_target_pairs={{0,3},{1,0},{2,1},{3,2},{4,7},{5,4},{6,5},{7,6},{8,11},{9,8},{10,9... | collective-permute-start | bytes 98312 | tf_op jit(solution)/shard_map/ppermute | solution.py:60
  116.8 1.3 collective-permute-start.16
  118.0 18.7 %factor.1.linv = bf16[512,512]{1,0:T(8,128)(2,1)S(1)} custom-call(s32[2]{0:T(128)S(1)} %copy-done.5, f32[16,40,128]{2,1,0:T(8,128)S(1)} %all-to-all-done.1.mine, f32[16,40,128]{2,1,0:T(8,128)S(1)} %collective-permute-done.9.other), custom_call_target="tpu_custom_call" | custom-call | flops 134217728 | bytes 3145728 | tf_op jit(solution)/shard_map/factor/pallas_call | solution.py:384
  136.8 3.5 %ortho.1 = (bf16[2048,128]{1,0:T(8,128)(2,1)S(1)}, bf16[2048,128]{1,0:T(8,128)(2,1)}, bf16[2048,128]{1,0:T(8,128)(2,1)}, bf16[2048,128]{1,0:T(8,128)(2,1)}) custom-call(s32[2]{0:T(128)S(1)} %copy-done.5, bf16[512,512]{1,0:T(8,128)(2,1)S(1)} %factor.1.linv, bf16[2048,512]{1,0:T(8,128)(2,1)S(1)} %copy-done.1), custom_call_target="tpu_custom_call" | custom-call | flops 1073741824 | bytes 4194304 | tf_op jit(solution)/shard_map/ortho/pallas_call | solution.py:415
  140.4 2.0 %collective-permute-start.10 = (bf16[2048,128]{1,0:T(8,128)(2,1)}, bf16[2048,128]{1,0:T(8,128)(2,1)S(1)}, u32[]{:S(2)}, u32[]{:S(2)}) collective-permute-start(bf16[2048,128]{1,0:T(8,128)(2,1)} %get-tuple-element.17), channel_id=1, source_target_pairs={{0,1},{1,2},{2,3},{3,0},{4,5},{5,6},{6,7},{7,4},{8,9},{9,10},{10,1... | collective-permute-start | bytes 1572872 | tf_op jit(solution)/shard_map/ppermute | solution.py:60
  143.0 1.8 %collective-permute-start.12 = (bf16[2048,128]{1,0:T(8,128)(2,1)}, bf16[2048,128]{1,0:T(8,128)(2,1)S(1)}, u32[]{:S(2)}, u32[]{:S(2)}) collective-permute-start(bf16[2048,128]{1,0:T(8,128)(2,1)} %get-tuple-element.19), channel_id=1, source_target_pairs={{0,3},{1,0},{2,1},{3,2},{4,7},{5,4},{6,5},{7,6},{8,11},{9,8},{10,9... | collective-permute-start | bytes 1572872 | tf_op jit(solution)/shard_map/ppermute | solution.py:60
  145.4 2.6 %tail.1 = f32[16,128]{1,0:T(8,128)} custom-call(s32[2]{0:T(128)} %pad_add_fusion.meta, bf16[512,512]{1,0:T(8,128)(2,1)} %copy-done.2, f32[64,128]{1,0:T(8,128)} %add_add_fusion.moment), custom_call_target="tpu_custom_call" | custom-call | flops 6291456 | bytes 524288 | tf_op jit(solution)/shard_map/tail/pallas_call | solution.py:471
  148.0 0.7 broadcast_in_dim.5
  148.7 10.2 %all_to_all.20.mine = f32[16,16,128]{2,1,0:T(8,128)S(1)} all-to-all(f32[16,16,128]{2,1,0:T(8,128)S(1)} %broadcast_in_dim.5), channel_id=1, replica_groups={{0,8,16,24,32,40,48,56,64,72,80,88,96,104,112,120},{4,12,20,28,36,44,52..., dimensions={0} | all-to-all | bytes 262144 | tf_op jit(solution)/shard_map/all_to_all | solution.py:56
  158.9 4.4 %collective-permute-start.19 = (f32[16,16,128]{2,1,0:T(8,128)S(1)}, f32[16,16,128]{2,1,0:T(8,128)S(1)}, u32[]{:S(2)}, u32[]{:S(2)}) collective-permute-start(f32[16,16,128]{2,1,0:T(8,128)S(1)} %all_to_all.20.mine), channel_id=1, source_target_pairs={{0,4},{4,0},{8,12},{12,8},{16,20},{20,16},{24,28},{28,24},{32,36},... | collective-permute-start | bytes 393224 | tf_op jit(solution)/shard_map/ppermute | solution.py:49
  163.3 1.0 collective-permute-done.19.other
  164.9 3.1 %project.1 = f32[512,128]{1,0:T(8,128)} custom-call(s32[2]{0:T(128)} %pad_add_fusion.meta, bf16[512,512]{1,0:T(8,128)(2,1)} %copy-done.2, f32[16,16,128]{2,1,0:T(8,128)} %copy-done.9, f32[16,16,128]{2,1,0:T(8,128)} %copy-done.13), custom_call_target="tpu_custom_call" | custom-call | flops 201326592 | bytes 1048576 | tf_op jit(solution)/shard_map/project/pallas_call | solution.py:493
  168.0 2.0 %join.1 = bf16[8192,128]{1,0:T(8,128)(2,1)} custom-call(s32[2]{0:T(128)S(1)} %copy-done.6, bf16[2048,128]{1,0:T(8,128)(2,1)S(1)} %get-tuple-element.16.refs_0_, bf16[2048,128]{1,0:T(8,128)(2,1)S(1)} %collective-permute-done.10.refs_1_, bf16[2048,128]{1,0:T(8,128)(2,1)S(1)} %collective-permute-done.11.refs_2_, ...), custom_call_target="tpu_custom_call" | custom-call | bytes 4194304 | tf_op jit(solution)/shard_map/join/pallas_call | solution.py:440
  (48 shorter events, 5.2 us)
Async XLA Ops:
  1.5 7.5 %collective-permute-start.1 = (bf16[256,128]{1,0:T(8,128)(2,1)S(1)}, bf16[256,128]{1,0:T(8,128)(2,1)S(1)}, u32[]{:S(2)}, u32[]{:S(2)}) collective-permute-start(bf16[256,128]{1,0:T(8,128)(2,1)S(1)} %get-tuple-element.24), channel_id=1, source_target_pairs={{4,0},{8,4},{12,8},{16,12},{20,16},{24,20},{28,24},{32,28},{36,32}... | collective-permute-start | bytes 196616 | tf_op jit(solution)/shard_map/ppermute | solution.py:516
  4.9 4.8 %collective-permute-start = (bf16[256,128]{1,0:T(8,128)(2,1)S(1)}, bf16[256,128]{1,0:T(8,128)(2,1)S(1)}, u32[]{:S(2)}, u32[]{:S(2)}) collective-permute-start(bf16[256,128]{1,0:T(8,128)(2,1)S(1)} %get-tuple-element.25), channel_id=1, source_target_pairs={{0,4},{4,8},{8,12},{12,16},{16,20},{20,24},{24,28},{28,32},{32,36}... | collective-permute-start | bytes 196616 | tf_op jit(solution)/shard_map/ppermute | solution.py:515
  9.0 0.7 copy-start.7
  9.7 0.6 copy-start.8
  15.0 19.1 %collective-permute-start.2 = (bf16[2048,128]{1,0:T(8,128)(2,1)}, bf16[2048,128]{1,0:T(8,128)(2,1)S(1)}, u32[]{:S(2)}, u32[]{:S(2)}) collective-permute-start(bf16[2048,128]{1,0:T(8,128)(2,1)} %op1.1), channel_id=1, source_target_pairs={{0,1},{1,2},{2,3},{3,0},{4,5},{5,6},{6,7},{7,4},{8,9},{9,10},{10,1... | collective-permute-start | bytes 1572872 | tf_op jit(solution)/shard_map/ppermute | solution.py:60
  21.0 20.9 %collective-permute-start.3 = (bf16[2048,128]{1,0:T(8,128)(2,1)}, bf16[2048,128]{1,0:T(8,128)(2,1)S(1)}, u32[]{:S(2)}, u32[]{:S(2)}) collective-permute-start(bf16[2048,128]{1,0:T(8,128)(2,1)} %op2.1), channel_id=1, source_target_pairs={{0,2},{1,3},{2,0},{3,1},{4,6},{5,7},{6,4},{7,5},{8,10},{9,11},{10,... | collective-permute-start | bytes 1572872 | tf_op jit(solution)/shard_map/ppermute | solution.py:60
  28.2 17.9 %copy-start.4 = (s32[2]{0:T(128)S(1)}, s32[2]{0:T(128)}, u32[]{:S(2)}) copy-start(s32[2]{0:T(128)} %pad_add_fusion.meta) | copy-start | bytes 28
  28.2 17.9 %collective-permute-start.4 = (bf16[2048,128]{1,0:T(8,128)(2,1)}, bf16[2048,128]{1,0:T(8,128)(2,1)S(1)}, u32[]{:S(2)}, u32[]{:S(2)}) collective-permute-start(bf16[2048,128]{1,0:T(8,128)(2,1)} %op3.1), channel_id=1, source_target_pairs={{0,3},{1,0},{2,1},{3,2},{4,7},{5,4},{6,5},{7,6},{8,11},{9,8},{10,9... | collective-permute-start | bytes 1572872 | tf_op jit(solution)/shard_map/ppermute | solution.py:60
  46.1 1.0 copy-start.3
  49.6 1.3 copy-start
  50.9 1.6 collective-permute-start.5
  53.3 17.8 %all-to-all-start = ((f32[16,40,128]{2,1,0:T(8,128)}), f32[16,40,128]{2,1,0:T(8,128)S(1)}, u32[]{:S(2)}, u32[]{:S(2)}) async-start(f32[16,40,128]{2,1,0:T(8,128)} %bitcast.2), calls=%async_computation | async-start | bytes 655360 | tf_op jit(solution)/shard_map/all_to_all | solution.py:56
  63.1 20.7 %collective-permute-start.13 = (bf16[256,512]{1,0:T(8,128)(2,1)S(1)}, bf16[256,512]{1,0:T(8,128)(2,1)S(1)}, u32[]{:S(2)}, u32[]{:S(2)}) collective-permute-start(bf16[256,512]{1,0:T(8,128)(2,1)S(1)} %get-tuple-element.20), channel_id=1, source_target_pairs={{0,1},{1,2},{2,3},{3,4},{4,5},{5,6},{6,7},{7,8},{8,9},{9,10},{10,1... | collective-permute-start | bytes 786440 | tf_op jit(solution)/shard_map/ppermute | solution.py:65
  67.4 16.4 %collective-permute-start.14 = (bf16[256,512]{1,0:T(8,128)(2,1)S(1)}, bf16[256,512]{1,0:T(8,128)(2,1)S(1)}, u32[]{:S(2)}, u32[]{:S(2)}) collective-permute-start(bf16[256,512]{1,0:T(8,128)(2,1)S(1)} %get-tuple-element.21), channel_id=1, source_target_pairs={{1,0},{2,1},{3,2},{4,3},{5,4},{6,5},{7,6},{8,7},{9,8},{10,9},{11,1... | collective-permute-start | bytes 786440 | tf_op jit(solution)/shard_map/ppermute | solution.py:65
  71.1 5.6 %collective-permute-start.8 = (f32[40,128]{1,0:T(8,128)S(1)}, f32[40,128]{1,0:T(8,128)S(1)}, u32[]{:S(2)}, u32[]{:S(2)}) collective-permute-start(f32[40,128]{1,0:T(8,128)S(1)} %reduce_sum.18), channel_id=1, source_target_pairs={{0,3},{1,0},{2,1},{3,2},{4,7},{5,4},{6,5},{7,6},{8,11},{9,8},{10,9... | collective-permute-start | bytes 61448 | tf_op jit(solution)/shard_map/ppermute | solution.py:60
  73.7 3.8 %collective-permute-start.7 = (f32[40,128]{1,0:T(8,128)S(1)}, f32[40,128]{1,0:T(8,128)S(1)}, u32[]{:S(2)}, u32[]{:S(2)}) collective-permute-start(f32[40,128]{1,0:T(8,128)S(1)} %reduce_sum.18), channel_id=1, source_target_pairs={{0,1},{1,2},{2,3},{3,0},{4,5},{5,6},{6,7},{7,4},{8,9},{9,10},{10,1... | collective-permute-start | bytes 61448 | tf_op jit(solution)/shard_map/ppermute | solution.py:60
  73.7 4.1 %collective-permute-start.6 = (f32[40,128]{1,0:T(8,128)S(1)}, f32[40,128]{1,0:T(8,128)S(1)}, u32[]{:S(2)}, u32[]{:S(2)}) collective-permute-start(f32[40,128]{1,0:T(8,128)S(1)} %reduce_sum.18), channel_id=1, source_target_pairs={{0,2},{1,3},{2,0},{3,1},{4,6},{5,7},{6,4},{7,5},{8,10},{9,11},{10,... | collective-permute-start | bytes 61448 | tf_op jit(solution)/shard_map/ppermute | solution.py:60
  78.6 21.4 %all-to-all-start.1 = ((f32[16,40,128]{2,1,0:T(8,128)}), f32[16,40,128]{2,1,0:T(8,128)S(1)}, u32[]{:S(2)}, u32[]{:S(2)}) async-start(f32[16,40,128]{2,1,0:T(8,128)} %broadcast_in_dim.4), calls=%async_computation.1 | async-start | bytes 655360 | tf_op jit(solution)/shard_map/all_to_all | solution.py:56
  83.8 0.7 copy-start.10
  83.8 0.8 copy-start.11
  84.6 33.4 %copy-start.5 = (s32[2]{0:T(128)S(1)}, s32[2]{0:T(128)}, u32[]{:S(2)}) copy-start(s32[2]{0:T(128)} %pad_add_fusion.meta) | copy-start | bytes 28
  84.6 52.2 %copy-start.1 = (bf16[2048,512]{1,0:T(8,128)(2,1)S(1)}, bf16[2048,512]{1,0:T(8,128)(2,1)}, u32[]{:S(2)}) copy-start(bf16[2048,512]{1,0:T(8,128)(2,1)} %copy-done) | copy-start | bytes 6291460
  93.0 4.4 %collective-permute-start.15 = (bf16[256,512]{1,0:T(8,128)(2,1)}, bf16[256,512]{1,0:T(8,128)(2,1)S(1)}, u32[]{:S(2)}, u32[]{:S(2)}) collective-permute-start(bf16[256,512]{1,0:T(8,128)(2,1)} %get-tuple-element.23), channel_id=1, source_target_pairs={{0,4},{4,0},{8,12},{12,8},{16,20},{20,16},{24,28},{28,24},{32,36},... | collective-permute-start | bytes 786440 | tf_op jit(solution)/shard_map/ppermute | solution.py:49
  97.4 0.7 copy-start.12
  100.0 68.1 %copy-start.6 = (s32[2]{0:T(128)S(1)}, s32[2]{0:T(128)}, u32[]{:S(2)}) copy-start(s32[2]{0:T(128)} %pad_add_fusion.meta) | copy-start | bytes 28
  100.0 14.5 %all-to-all-start.2 = ((bf16[16,64,128]{2,1,0:T(8,128)(2,1)}), bf16[16,64,128]{2,1,0:T(8,128)(2,1)S(1)}, u32[]{:S(2)}, u32[]{:S(2)}) async-start(bf16[16,64,128]{2,1,0:T(8,128)(2,1)} %pack.1), calls=%async_computation.2 | async-start | bytes 524288 | tf_op jit(solution)/shard_map/all_to_all | solution.py:56
  106.9 11.1 %collective-permute-start.9 = (f32[16,40,128]{2,1,0:T(8,128)S(1)}, f32[16,40,128]{2,1,0:T(8,128)S(1)}, u32[]{:S(2)}, u32[]{:S(2)}) collective-permute-start(f32[16,40,128]{2,1,0:T(8,128)S(1)} %all-to-all-done.1.mine), channel_id=1, source_target_pairs={{0,4},{4,0},{8,12},{12,8},{16,20},{20,16},{24,28},{28,24},{32,36},... | collective-permute-start | bytes 983048 | tf_op jit(solution)/shard_map/ppermute | solution.py:49
  114.5 28.5 %collective-permute-start.18 = (f32[64,128]{1,0:T(8,128)S(1)}, f32[64,128]{1,0:T(8,128)S(1)}, u32[]{:S(2)}, u32[]{:S(2)}) collective-permute-start(f32[64,128]{1,0:T(8,128)S(1)} %convert_reduce_fusion), channel_id=1, source_target_pairs={{0,3},{1,0},{2,1},{3,2},{4,7},{5,4},{6,5},{7,6},{8,11},{9,8},{10,9... | collective-permute-start | bytes 98312 | tf_op jit(solution)/shard_map/ppermute | solution.py:60
  116.8 28.0 %collective-permute-start.17 = (f32[64,128]{1,0:T(8,128)S(1)}, f32[64,128]{1,0:T(8,128)S(1)}, u32[]{:S(2)}, u32[]{:S(2)}) collective-permute-start(f32[64,128]{1,0:T(8,128)S(1)} %convert_reduce_fusion), channel_id=1, source_target_pairs={{0,1},{1,2},{2,3},{3,0},{4,5},{5,6},{6,7},{7,4},{8,9},{9,10},{10,1... | collective-permute-start | bytes 98312 | tf_op jit(solution)/shard_map/ppermute | solution.py:60
  116.8 28.0 %collective-permute-start.16 = (f32[64,128]{1,0:T(8,128)S(1)}, f32[64,128]{1,0:T(8,128)S(1)}, u32[]{:S(2)}, u32[]{:S(2)}) collective-permute-start(f32[64,128]{1,0:T(8,128)S(1)} %convert_reduce_fusion), channel_id=1, source_target_pairs={{0,2},{1,3},{2,0},{3,1},{4,6},{5,7},{6,4},{7,5},{8,10},{9,11},{10,... | collective-permute-start | bytes 98312 | tf_op jit(solution)/shard_map/ppermute | solution.py:60
  136.8 8.6 %copy-start.2 = (bf16[512,512]{1,0:T(8,128)(2,1)}, bf16[512,512]{1,0:T(8,128)(2,1)S(1)}, u32[]{:S(2)}) copy-start(bf16[512,512]{1,0:T(8,128)(2,1)S(1)} %factor.1.linv) | copy-start | bytes 1572868
  140.4 27.7 %collective-permute-start.10 = (bf16[2048,128]{1,0:T(8,128)(2,1)}, bf16[2048,128]{1,0:T(8,128)(2,1)S(1)}, u32[]{:S(2)}, u32[]{:S(2)}) collective-permute-start(bf16[2048,128]{1,0:T(8,128)(2,1)} %get-tuple-element.17), channel_id=1, source_target_pairs={{0,1},{1,2},{2,3},{3,0},{4,5},{5,6},{6,7},{7,4},{8,9},{9,10},{10,1... | collective-permute-start | bytes 1572872 | tf_op jit(solution)/shard_map/ppermute | solution.py:60
  142.4 25.7 %collective-permute-start.11 = (bf16[2048,128]{1,0:T(8,128)(2,1)}, bf16[2048,128]{1,0:T(8,128)(2,1)S(1)}, u32[]{:S(2)}, u32[]{:S(2)}) collective-permute-start(bf16[2048,128]{1,0:T(8,128)(2,1)} %get-tuple-element.18), channel_id=1, source_target_pairs={{0,2},{1,3},{2,0},{3,1},{4,6},{5,7},{6,4},{7,5},{8,10},{9,11},{10,... | collective-permute-start | bytes 1572872 | tf_op jit(solution)/shard_map/ppermute | solution.py:60
  143.0 25.0 %collective-permute-start.12 = (bf16[2048,128]{1,0:T(8,128)(2,1)}, bf16[2048,128]{1,0:T(8,128)(2,1)S(1)}, u32[]{:S(2)}, u32[]{:S(2)}) collective-permute-start(bf16[2048,128]{1,0:T(8,128)(2,1)} %get-tuple-element.19), channel_id=1, source_target_pairs={{0,3},{1,0},{2,1},{3,2},{4,7},{5,4},{6,5},{7,6},{8,11},{9,8},{10,9... | collective-permute-start | bytes 1572872 | tf_op jit(solution)/shard_map/ppermute | solution.py:60
  158.9 5.3 %copy-start.9 = (f32[16,16,128]{2,1,0:T(8,128)}, f32[16,16,128]{2,1,0:T(8,128)S(1)}, u32[]{:S(2)}) copy-start(f32[16,16,128]{2,1,0:T(8,128)S(1)} %all_to_all.20.mine) | copy-start | bytes 393220
  158.9 5.3 %collective-permute-start.19 = (f32[16,16,128]{2,1,0:T(8,128)S(1)}, f32[16,16,128]{2,1,0:T(8,128)S(1)}, u32[]{:S(2)}, u32[]{:S(2)}) collective-permute-start(f32[16,16,128]{2,1,0:T(8,128)S(1)} %all_to_all.20.mine), channel_id=1, source_target_pairs={{0,4},{4,0},{8,12},{12,8},{16,20},{20,16},{24,28},{28,24},{32,36},... | collective-permute-start | bytes 393224 | tf_op jit(solution)/shard_map/ppermute | solution.py:49
  164.3 0.6 copy-start.13
